TPU v7x, 32 devices: a whole 2x2x4 slice. The times are simulated.
32 devices in a mesh: mem: 4 (over y, x), tt: 8 (over z, core).
Axes of the slice: x: 2, y: 2, z: 4, core: 2. Of those that a mesh axis runs over, the one named last changes fastest.
Arguments:
- history: bfloat16 [2, 16, 128, 16, 128], P(None, 'mem', None, 'tt'), may hold values from -0.125 to 0.125
- free_rows: bfloat16 [2, 2, 128, 16, 128], P(None, None, None, 'tt'), may hold values from -3 to 3
- memory_start: int32 [2], replicated, may hold values from 0 to 7, as said below
- now: int32 [1], replicated, may hold values from 8 to 14
Outputs:
- new_rows: bfloat16 [2, 2, 128, 16, 128], P(None, None, None, 'tt')
Inputs may be any that keep to these rules, and one draw needn't show every extreme that they name: Row r's memory integral starts at memory_start[r]; starts need not be distinct, and some row starts at the largest allowed value. The new rows' times now + r lie inside the grid.
All inputs are finite; a program needn't handle non-finite values.
Results may differ from a plain program's by a relative error of at most 0.012.
The roundings to bfloat16 on the way count: a program that leaves them out, or rounds other values in their place, can miss the bound.
Values may be sent and summed in bfloat16 or wider, within the bound.
No kernel may reach another device: no remote copies, remote signals or barrier semaphores. Data moves between devices by JAX's collectives and lax.ppermute only.
A program may use at most 64 MiB of HBM per device.

v0:
```python
import jax
import jax.numpy as jnp
from jax import lax
from jax.sharding import PartitionSpec as P

ITERS = 3


COUPLING = 0.5


def from_root(value, axis, source):
    kept = jnp.where(lax.axis_index(axis) == source, value, 0).astype(value.dtype)
    return lax.psum(kept, axis)


def self_energy(columns, live_weight):
    real_part = columns[0].astype(jnp.float32)
    imag_part = columns[1].astype(jnp.float32)
    modulus = real_part * real_part + imag_part * imag_part
    sig_real = (-(real_part * modulus) * live_weight).astype(jnp.bfloat16)
    sig_imag = (-(imag_part * modulus) * live_weight).astype(jnp.bfloat16)
    return (sig_real, sig_imag)


def memory_integral(sig_real, sig_imag, hist_real, hist_imag):
    out_real = jnp.dot(sig_real, hist_real, preferred_element_type=jnp.float32) - jnp.dot(
        sig_imag, hist_imag, preferred_element_type=jnp.float32
    )
    out_imag = jnp.dot(sig_real, hist_imag, preferred_element_type=jnp.float32) + jnp.dot(
        sig_imag, hist_real, preferred_element_type=jnp.float32
    )
    return jnp.stack([out_real, out_imag])


def on_device(history, free_rows, memory_start, now):
    tiles_per_mem = lax.axis_size("tt") // lax.axis_size("mem")
    row_count = free_rows.shape[1]
    orb_count = free_rows.shape[2]
    col_count = free_rows.shape[3]
    span_count = history.shape[1]
    hist_real = history[0].reshape(span_count * orb_count, col_count * orb_count)
    hist_imag = history[1].reshape(span_count * orb_count, col_count * orb_count)
    mem_index = lax.axis_index("mem")
    mem_times = mem_index * span_count + jnp.arange(span_count, dtype=jnp.int32)
    row_time = now[0] + jnp.arange(row_count, dtype=jnp.int32)
    live_mask = (mem_times[None, :] >= memory_start[:, None]) & (
        mem_times[None, :] < row_time[:, None]
    )
    live_weight = live_mask.astype(jnp.float32)[:, None, :, None]
    free_flat = free_rows.astype(jnp.float32).reshape(
        2, row_count * orb_count, col_count * orb_count
    )
    current = free_rows
    for sweep in range(ITERS):
        pieces = []
        for source in range(tiles_per_mem):
            pieces.append(from_root(current, "tt", mem_index * tiles_per_mem + source))
        columns = jnp.concatenate(pieces, axis=3)
        sig_real, sig_imag = self_energy(columns, live_weight)
        flat_real = sig_real.reshape(row_count * orb_count, span_count * orb_count)
        flat_imag = sig_imag.reshape(row_count * orb_count, span_count * orb_count)
        partial_value = memory_integral(flat_real, flat_imag, hist_real, hist_imag)
        row_share = lax.psum_scatter(partial_value, "mem", scatter_dimension=1, tiled=True)
        share_width = row_share.shape[1]
        free_share = lax.dynamic_slice_in_dim(free_flat, mem_index * share_width, share_width, 1)
        updated = (free_share + COUPLING * row_share).astype(jnp.bfloat16)
        current = lax.all_gather(updated, "mem", axis=1, tiled=True).reshape(free_rows.shape)
    return current


def solution(mesh):
    return jax.shard_map(
        on_device,
        mesh=mesh,
        in_specs=(P(None, "mem", None, "tt", None), P(None, None, None, "tt", None), P(), P()),
        out_specs=P(None, None, None, "tt", None),
        check_vma=False,
    )
```

profile of v0, /device:TPU:0, one launch (start us, length us, event | category | flops | bytes accessed | tf_op | source)
XLA Modules:
  0.0 309.3 jit_solution(9752391792223275087)
XLA Ops:
  6.5 2.2 broadcast_select_fusion.1
  10.6 58.5 %all-reduce.11.cloned.1.call-done = (bf16[2,2,128,2,128]{4,3,2,1,0:T(2,128)(2,1)}, bf16[2,2,128,2,128]{4,3,2,1,0:T(2,128)(2,1)}) async-done(((bf16[2,2,128,2,128]{4,3,2,1,0:T(2,128)(2,1)}, bf16[2,2,128,2,128]{4,3,2,1,0:T(2,128)(2,1)}), (bf16[2,2,128,2,128]{4,3,2,1,0:T(2,128)(2,1)}, bf16[2,2,128,2,128]{4,3,2,1,0:T(2,128)(2,1)})) %all-reduce.11.cloned.1.call-update) | async-done | bytes 524304 | tf_op jit(solution)/shard_map/psum | solution.py:14
  69.1 2.4 fusion.12
  72.4 0.8 pad_maximum_fusion
  73.3 0.9 copy-done
  74.4 23.3 %reduce-scatter.4.cloned.1.call-done = f32[2,64,256]{2,1,0:T(8,128)} async-done(((f32[2,256,256]{2,1,0:T(8,128)}), f32[2,64,256]{2,1,0:T(8,128)}) %reduce-scatter.4.cloned.1.call-update) | async-done | bytes 131088 | tf_op jit(solution)/shard_map/reduce_scatter | solution.py:64
  97.6 0.9 add_convert_fusion.2
  98.5 9.2 %all_gather.9 = bf16[2,256,256]{2,1,0:T(8,128)(2,1)S(1)} all-gather(bf16[2,64,256]{2,1,0:T(8,128)(2,1)S(1)} %add_convert_fusion.2), channel_id=1, replica_groups=mesh['mem'=4,'tt'=8] {'mem'}, dimensions={1}, use_global_device_ids=true | all-gather | bytes 327680 | tf_op jit(solution)/shard_map/all_gather | solution.py:68
  107.8 0.8 select_n.58
  108.6 0.8 select_n.61
  109.4 56.6 %all-reduce.9.cloned.1.call-done = (bf16[2,2,128,2,128]{4,3,2,1,0:T(2,128)(2,1)}, bf16[2,2,128,2,128]{4,3,2,1,0:T(2,128)(2,1)}) async-done(((bf16[2,2,128,2,128]{4,3,2,1,0:T(2,128)(2,1)}, bf16[2,2,128,2,128]{4,3,2,1,0:T(2,128)(2,1)}), (bf16[2,2,128,2,128]{4,3,2,1,0:T(2,128)(2,1)}, bf16[2,2,128,2,128]{4,3,2,1,0:T(2,128)(2,1)})) %all-reduce.9.cloned.1.call-update) | async-done | bytes 524304 | tf_op jit(solution)/shard_map/psum | solution.py:14
  166.1 2.4 fusion.19
  169.4 0.8 pad_maximum_fusion.1
  170.3 24.3 %reduce-scatter.6.cloned.1.call-done = f32[2,64,256]{2,1,0:T(8,128)} async-done(((f32[2,256,256]{2,1,0:T(8,128)}), f32[2,64,256]{2,1,0:T(8,128)}) %reduce-scatter.6.cloned.1.call-update) | async-done | bytes 131088 | tf_op jit(solution)/shard_map/reduce_scatter | solution.py:64
  194.6 0.9 add_convert_fusion.1
  195.5 9.2 %all_gather.10 = bf16[2,256,256]{2,1,0:T(8,128)(2,1)S(1)} all-gather(bf16[2,64,256]{2,1,0:T(8,128)(2,1)S(1)} %add_convert_fusion.1), channel_id=1, replica_groups=mesh['mem'=4,'tt'=8] {'mem'}, dimensions={1}, use_global_device_ids=true | all-gather | bytes 327680 | tf_op jit(solution)/shard_map/all_gather | solution.py:68
  204.8 0.8 select_n.63
  206.4 56.7 %all-reduce.7.cloned.1.call-done = (bf16[2,2,128,2,128]{4,3,2,1,0:T(2,128)(2,1)}, bf16[2,2,128,2,128]{4,3,2,1,0:T(2,128)(2,1)}) async-done(((bf16[2,2,128,2,128]{4,3,2,1,0:T(2,128)(2,1)}, bf16[2,2,128,2,128]{4,3,2,1,0:T(2,128)(2,1)}), (bf16[2,2,128,2,128]{4,3,2,1,0:T(2,128)(2,1)}, bf16[2,2,128,2,128]{4,3,2,1,0:T(2,128)(2,1)})) %all-reduce.7.cloned.1.call-update) | async-done | bytes 524304 | tf_op jit(solution)/shard_map/psum | solution.py:14
  263.0 2.4 fusion.26
  266.3 0.8 pad_maximum_fusion.2
  267.2 24.3 %reduce-scatter.8.cloned.1.call-done = f32[2,64,256]{2,1,0:T(8,128)} async-done(((f32[2,256,256]{2,1,0:T(8,128)}), f32[2,64,256]{2,1,0:T(8,128)}) %reduce-scatter.8.cloned.1.call-update) | async-done | bytes 131088 | tf_op jit(solution)/shard_map/reduce_scatter | solution.py:64
  291.5 0.9 add_convert_fusion
  292.4 9.3 %all_gather.11 = bf16[2,256,256]{2,1,0:T(8,128)(2,1)S(1)} all-gather(bf16[2,64,256]{2,1,0:T(8,128)(2,1)S(1)} %add_convert_fusion), channel_id=1, replica_groups=mesh['mem'=4,'tt'=8] {'mem'}, dimensions={1}, use_global_device_ids=true | all-gather | bytes 327680 | tf_op jit(solution)/shard_map/all_gather | solution.py:68
  301.7 0.8 reshape.321
  (37 shorter events, 5.2 us)
Async XLA Ops:
  6.5 62.6 %all-reduce.11.cloned.1.call-start = ((), (), s32[]{:S(2)}) async-start(), calls=%async_computation.8 | async-start | bytes 1048576 | tf_op jit(solution)/shard_map/psum | solution.py:14
  6.5 3.7 %copy-start.1 = (bf16[2,4,128,2,128]{4,3,2,1,0:T(2,128)(2,1)S(1)}, bf16[2,4,128,2,128]{4,3,2,1,0:T(2,128)(2,1)}, u32[]{:S(2)}) copy-start(bf16[2,4,128,2,128]{4,3,2,1,0:T(2,128)(2,1)} %param.4) | copy-start | bytes 1572868
  8.8 88.9 %reduce-scatter.4.cloned.1.call-start = ((), (), s32[]{:S(2)}) async-start(), calls=%async_computation.3 | async-start | bytes 655360 | tf_op jit(solution)/shard_map/reduce_scatter | solution.py:64
  9.5 0.7 copy-start.2
  73.3 0.9 copy-start
  73.3 92.8 %all-reduce.9.cloned.1.call-start = ((), (), s32[]{:S(2)}) async-start(), calls=%async_computation.7 | async-start | bytes 1048576 | tf_op jit(solution)/shard_map/psum | solution.py:14
  109.4 85.2 %reduce-scatter.6.cloned.1.call-start = ((), (), s32[]{:S(2)}) async-start(), calls=%async_computation.4 | async-start | bytes 655360 | tf_op jit(solution)/shard_map/reduce_scatter | solution.py:64
  170.2 92.8 %all-reduce.7.cloned.1.call-start = ((), (), s32[]{:S(2)}) async-start(), calls=%async_computation.6 | async-start | bytes 1048576 | tf_op jit(solution)/shard_map/psum | solution.py:14
  206.3 85.2 %reduce-scatter.8.cloned.1.call-start = ((), (), s32[]{:S(2)}) async-start(), calls=%async_computation.5 | async-start | bytes 655360 | tf_op jit(solution)/shard_map/reduce_scatter | solution.py:64
Sparse Core Ops, SparseCore 0:
  9.7 59.3 all-reduce.10
  73.4 24.1 reduce-scatter.3
  109.5 56.5 all-reduce.8
  170.3 24.1 reduce-scatter.5
  206.4 56.5 all-reduce.6
  267.3 24.1 reduce-scatter.7
where the time goes:
time: 310 us; the launch traced here: 309 us
  waiting for transfers between devices  244 us (79%)
  blocking collectives  27.7 us (9%)
  other arithmetic  14.7 us (5%)
  between operations  14.3 us (5%)
  local copies, waits for them, and re-layouts  5.86 us (2%)
    psum x3, waiting for transfers between devices, from_root(): return lax.psum(kept, axis)  172 us
    reduce_scatter x3, waiting for transfers between devices, on_device(): lax.psum_scatter(partial_value, 'mem', scatter_dimension=1, tiled=True)  71.8 us
    all_gather x3, blocking collectives, on_device(): lax.all_gather(updated, 'mem', axis=1, tiled=True).reshape(free_rows.shape)  27.7 us
    convert_element_type x3, other arithmetic, self_energy(): sig_imag = (-(imag_part * modulus) * live_weight).astype(jnp.bfloat16)  7.07 us
  transfers between devices with their start and end apart: 6, of which 6 were waited for; matrix products, arithmetic and copies ran while one was open for 0% of the time, Pallas kernels for 0%

commit v1 on v0

v1 whole, which is shorter than its diff:
```python
import functools

import jax
import jax.numpy as jnp
from jax import lax
from jax.experimental import pallas as pl
from jax.experimental.pallas import tpu as pltpu
from jax.sharding import PartitionSpec as P


ITERS = 3
COUPLING = 0.5
VMEM_LIMIT = 20 << 20
BOTH = ("mem", "tt")


def swap(value, mem_mask, tt_mask):
    n_mem, n_tt = lax.axis_size("mem"), lax.axis_size("tt")
    pairs = [(m * n_tt + t, (m ^ mem_mask) * n_tt + (t ^ tt_mask)) for m in range(n_mem) for t in range(n_tt)]
    return lax.ppermute(value, BOTH, pairs)


def call(kernel, out_shape, args, scratch=(), smem=0, unread=0):
    spaces = [pltpu.SMEM] * smem + [pltpu.VMEM] * (len(args) - smem - unread) + [pl.ANY] * unread
    vmem = pl.BlockSpec(memory_space=pltpu.VMEM)
    many = isinstance(out_shape, list)
    return pl.pallas_call(
        kernel,
        out_shape=[jax.ShapeDtypeStruct(s, d) for s, d in out_shape] if many else jax.ShapeDtypeStruct(*out_shape),
        in_specs=[pl.BlockSpec(memory_space=s) for s in spaces],
        out_specs=[vmem] * len(out_shape) if many else vmem,
        scratch_shapes=list(scratch),
        compiler_params=pltpu.CompilerParams(vmem_limit_bytes=VMEM_LIMIT),
    )(*args)


def rows_kernel(free_ref, keep_ref, give_ref):
    mem, core = lax.axis_index("mem"), lax.axis_index("tt") % 2
    for p in range(free_ref.shape[0]):
        for r in range(free_ref.shape[1]):
            keep_ref[p, r] = free_ref[p, r, mem, core]
            give_ref[p, r] = free_ref[p, r, mem, 1 - core]


def stack_kernel(a_ref, b_ref, out_ref):
    out_ref[0] = a_ref[...]
    out_ref[1] = b_ref[...]


def cut_kernel(at, ref, *refs):
    refs[-1][0] = ref[at]


def split_kernel(n_parts, *refs):
    parts, out_ref, wide = refs[:n_parts], refs[-2], refs[-1]
    spans, rows, lanes = out_ref.shape[1], out_ref.shape[2], wide.shape[2]
    cols = out_ref.shape[3] // lanes
    at = 0
    for ref in parts:
        for p in range(ref.shape[0]):
            for s in range(spans):
                slot = at * spans + s
                wide[slot] = ref[p, s].astype(jnp.float32)
                for c in range(cols):
                    picked = wide[slot, pl.ds(c, rows, stride=cols), :]
                    out_ref[at, s, :, c * lanes : (c + 1) * lanes] = picked.astype(jnp.bfloat16)
            at += 1


def split_history(parts):
    spans, rows, cols, lanes = parts[0].shape[1:]
    merged = [p.reshape(p.shape[0], spans, rows * cols, lanes) for p in parts]
    return call(
        functools.partial(split_kernel, len(parts)),
        ((2, spans, rows, cols * lanes), jnp.bfloat16),
        merged,
        [pltpu.VMEM((2 * spans, rows * cols, lanes), jnp.float32)],
    )


def put_sigma(tile, b, dims, start_ref, now_ref, wide, sig):
    row_count, orb_rows, cols, lanes = dims
    rows = row_count * orb_rows
    row_of = lax.broadcasted_iota(jnp.int32, (rows, lanes), 0) // orb_rows
    for p in range(2):
        wide[p] = tile[p].astype(jnp.float32)
    for c in range(cols):
        s = b * cols + c
        weight = jnp.zeros((rows, lanes), jnp.float32)
        for r in range(row_count):
            on = (s >= start_ref[r]) & (s < now_ref[0] + r)
            weight = jnp.where(row_of == r, jnp.where(on, 1.0, 0.0), weight)
        real = wide[0, pl.ds(c, rows, stride=cols), :]
        imag = wide[1, pl.ds(c, rows, stride=cols), :]
        modulus = real * real + imag * imag
        at = slice(c * lanes, (c + 1) * lanes)
        sig[:rows, at] = (-(real * modulus) * weight).astype(jnp.bfloat16)
        sig[rows:, at] = (-(imag * modulus) * weight).astype(jnp.bfloat16)


def accumulate(sums, left, hist, h, cols):
    at = slice(h * cols, (h + 1) * cols)
    depth = cols * hist.shape[2]
    return tuple(
        total + jnp.dot(left, hist[p, at].reshape(depth, hist.shape[3]), preferred_element_type=jnp.float32)
        for p, total in enumerate(sums)
    )


def as_complex(sums):
    rows = sums[0].shape[0] // 2
    return sums[0][:rows] - sums[1][rows:], sums[1][:rows] + sums[0][rows:]


def update(free, value, dims, wide, p):
    row_count, orb_rows, cols, lanes = dims
    rows = row_count * orb_rows
    for c in range(cols):
        wide[p, pl.ds(c, rows, stride=cols), :] = value[:, c * lanes : (c + 1) * lanes]
    return free.astype(jnp.float32) + COUPLING * wide[p]


def integral(tiles, hists, masks, dims, start_ref, now_ref, wide, sig):
    for k, (tile, block, place) in enumerate(tiles):
        put_sigma(tile, block, dims, start_ref, now_ref, wide.at[k], sig.at[place])
    zero = jnp.zeros((2 * dims[0] * dims[1], dims[2] * dims[3]), jnp.float32)
    sums = [(zero, zero), (zero, zero)]
    for i, mask in enumerate(masks):
        for h in range(2):
            left = sig[mask * 2 + h]
            pair = (hists[i], hists[len(masks) + i])
            sums = [accumulate(t, left, hist, h, dims[2]) for t, hist in zip(sums, pair)]
    return [as_complex(t) for t in sums]


def all_tiles(blocks):
    tt = lax.axis_index("tt")
    return [(block.at[e], tt ^ (2 * k + e), tt ^ (2 * k + e)) for k, block in enumerate(blocks) for e in range(2)]


def help_kernel(dims, lent, start_ref, now_ref, tile_ref, own, pair, out_ref, wide, sig):
    core = lax.axis_index("tt") % 2
    block = lax.axis_index("mem") ^ lent
    tiles = [(tile_ref.at[e], block * 2 + (core ^ e), core ^ e) for e in range(2)]
    for e, value in enumerate(integral(tiles, (own, pair), (0,), dims, start_ref, now_ref, wide, sig)):
        for p in range(2):
            out_ref[e, p] = value[p].astype(out_ref.dtype)


def near_kernel(dims, count, near, start_ref, now_ref, *refs):
    blocks, hists, (out_ref, wide, sig) = refs[:count], refs[count:-3], refs[-3:]
    masks = [lax.axis_index("mem") ^ q for q in near]
    for e, value in enumerate(integral(all_tiles(blocks), hists, masks, dims, start_ref, now_ref, wide, sig)):
        for p in range(2):
            out_ref[e, p] = value[p]


def first_kernel(dims, free_ref, near_ref, far_ref, *refs):
    out_ref, wide = refs[-2:]
    for e in range(2):
        for p in range(2):
            value = near_ref[e, p] + far_ref[e, p].astype(jnp.float32)
            out_ref[e, p] = update(free_ref[e, p], value, dims, wide.at[e], p).astype(out_ref.dtype)


def step_kernel(dims, count, n_mem, start_ref, now_ref, free_ref, *refs):
    blocks, hists, (out_ref, wide, sig) = refs[:count], refs[count:-3], refs[-3:]
    masks = [lax.axis_index("mem") ^ q for q in range(n_mem)]
    for e, value in enumerate(integral(all_tiles(blocks), hists, masks, dims, start_ref, now_ref, wide, sig)):
        for p in range(2):
            out_ref[e, p] = update(free_ref[e, p], value[p], dims, wide.at[e], p).astype(out_ref.dtype)


def pick_kernel(wanted, *refs):
    blocks, out_ref = refs[:-1], refs[-1]
    for k, block in enumerate(blocks):
        @pl.when((lax.axis_index("tt") ^ (2 * k)) // 2 == lax.axis_index("mem") ^ wanted)
        def _():
            out_ref[...] = block[...]


def join_kernel(row_count, *refs):
    blocks, out_ref = refs[:-1], refs[-1]
    mem, core = lax.axis_index("mem"), lax.axis_index("tt") % 2
    size = out_ref.shape[4]
    for k, ref in enumerate(blocks):
        for e in range(2):
            for p in range(2):
                for r in range(row_count):
                    out_ref[p, r, mem ^ k, core ^ e] = ref[e, p, r * size : (r + 1) * size, :]


def on_device(history, free_rows, memory_start, now):
    n_mem, n_tt = lax.axis_size("mem"), lax.axis_size("tt")
    if n_tt != 2 * n_mem:
        raise ValueError("unequal split")
    parts, row_count, orb_count, cols, lanes = free_rows.shape
    orb_rows = orb_count // n_mem
    bf16, f32 = jnp.bfloat16, jnp.float32
    live = (memory_start, now)
    dims = (row_count, orb_rows // 2, cols, lanes)
    rows = row_count * orb_rows // 2
    size = orb_rows * cols // 2
    evens = range(2, n_tt, 2)

    def stack(a, b):
        return call(stack_kernel, ((2, *a.shape), bf16), [a, b])

    def gather_current(own):
        blocks = [own] + [None] * len(evens)
        for k in reversed(evens):
            blocks[k // 2] = swap(own, 0, k)
        return blocks

    def scratch(count):
        return [
            pltpu.VMEM((count, 2, rows * cols, lanes), f32),
            pltpu.VMEM((count, 2 * rows, cols * lanes), bf16),
        ]

    raw = {0: history}
    for k in range(1, n_mem):
        if k & (k - 1) == 0:
            raw[k] = swap(history, k, 0)
    relayed = {}

    def part(k, p):
        if k in raw:
            return call(functools.partial(cut_kernel, p), ((1, *history.shape[1:4], lanes), bf16), [raw[k]])
        if (k, p) not in relayed:
            bit = 1 << (k.bit_length() - 1) if p else k & -k
            relayed[k, p] = swap(part(k ^ bit, p), bit, 0)
        return relayed[k, p]

    def parts_of(k):
        return (raw[k],) if k in raw else (part(k, 0), part(k, 1))

    keep, give = call(
        rows_kernel,
        [((parts, row_count, size, lanes), bf16)] * 2,
        [free_rows.reshape(parts, row_count, n_mem, 2, size, lanes)],
    )
    keep, give = (a.reshape(parts, rows * cols, lanes) for a in (keep, give))
    free = stack(keep, swap(give, 0, 1))
    blocks = gather_current(free)

    last, helper = n_mem - 1, 1
    lent = last ^ helper
    near = tuple(range(n_mem - 1))
    picked = call(functools.partial(pick_kernel, last), (free.shape, bf16), blocks)
    lent_block = swap(picked, helper, 0)
    split, pair = {}, {}
    for k in near:
        split[k] = split_history(parts_of(k))
        pair[k] = swap(split[k], 0, 1)
    lent_sum = call(
        functools.partial(help_kernel, dims, lent),
        ((2, parts, rows, cols * lanes), bf16),
        [*live, lent_block, split[lent], pair[lent]],
        scratch(2),
        smem=2,
    )
    last_sum = swap(lent_sum, helper, 0)
    near_sum = call(
        functools.partial(near_kernel, dims, len(blocks), near),
        ((2, parts, rows, cols * lanes), f32),
        [*live, *blocks, *(split[q] for q in near), *(pair[q] for q in near)],
        scratch(n_tt),
        smem=2,
    )
    current = call(
        functools.partial(first_kernel, dims),
        (free.shape, bf16),
        [free, near_sum, last_sum],
        [pltpu.VMEM((2, parts, rows * cols, lanes), f32)],
    )
    blocks = gather_current(current)
    split[last] = split_history(parts_of(last))
    pair[last] = swap(split[last], 0, 1)
    hists = [split[k] for k in range(n_mem)] + [pair[k] for k in range(n_mem)]
    for sweep in range(1, ITERS):
        current = call(
            functools.partial(step_kernel, dims, len(blocks), n_mem),
            (free.shape, bf16),
            [*live, free, *blocks, *hists],
            scratch(n_tt),
            smem=2,
        )
        if sweep < ITERS - 1:
            blocks = gather_current(current)
    own = stack(current[0], swap(current[1], 0, 1))
    others = [None] * n_mem
    for k in reversed(range(1, n_mem)):
        others[k] = swap(own, k, 0)
    out = call(
        functools.partial(join_kernel, row_count), ((parts, row_count, n_mem, 2, size, lanes), bf16), [own] + others[1:]
    )
    return out.reshape(free_rows.shape)


def solution(mesh):
    return jax.shard_map(
        on_device,
        mesh=mesh,
        in_specs=(P(None, "mem", None, "tt", None), P(None, None, None, "tt", None), P(), P()),
        out_specs=P(None, None, None, "tt", None),
        check_vma=False,
    )
```

time: 310 us -> 81.7 us (0.26)
  waiting for transfers between devices: 244 us -> 43.3 us
  starting transfers between devices: 0.21 us -> 29.1 us
  blocking collectives: 27.7 us -> 0 us
  other arithmetic: 14.7 us -> 0 us
  between operations: 14.3 us -> 0.78 us
  Pallas kernels: 0 us -> 6.77 us
  local copies, waits for them, and re-layouts: 5.86 us -> 1.48 us
    psum x3 -> x0, waiting for transfers between devices: 172 us -> none  [from_root(): return lax.psum(kept, axis)]
    reduce_scatter x3 -> x0, waiting for transfers between devices: 71.8 us -> none  [on_device(): lax.psum_scatter(partial_value, 'mem', scatter_dimension=1, tiled=True)]
    ppermute x0 -> x24, waiting for transfers between devices: none -> 43.3 us  [swap(): return lax.ppermute(value, BOTH, pairs)]
    ppermute x0 -> x24, starting transfers between devices: none -> 29.1 us  [swap(): return lax.ppermute(value, BOTH, pairs)]
    all_gather x3 -> x0, blocking collectives: 27.7 us -> none  [on_device(): lax.all_gather(updated, 'mem', axis=1, tiled=True).reshape(free_rows.shape)]
    convert_element_type x7 -> x0, other arithmetic: 9.9 us -> none  [the longest x3 7.07 us: self_energy(): sig_imag = (-(imag_part * modulus) * live_weight).astype(jnp.bfloat16)]
    pallas_call x0 -> x16, Pallas kernels: none -> 6.77 us  [call(): pl.pallas_call(kernel, out_shape=[jax.ShapeDtypeStruct(s, d) for s, d in...]
  transfers between devices with their start and end apart: 6 -> 24, of which waited for: 6 -> 17; matrix products, arithmetic and copies ran while one was open for 0% -> 0% of each run, Pallas kernels for 0% -> 4%
where the time goes in v1:
time: 81.7 us; the launch traced here: 81.5 us
  waiting for transfers between devices  43.3 us (53%)
  starting transfers between devices  29.1 us (36%)
  Pallas kernels  6.77 us (8%)
  local copies, waits for them, and re-layouts  1.48 us (2%)
    ppermute x24, waiting for transfers between devices, swap(): return lax.ppermute(value, BOTH, pairs)  43.3 us
    ppermute x24, starting transfers between devices, swap(): return lax.ppermute(value, BOTH, pairs)  29.1 us
    pallas_call x16, Pallas kernels, call(): pl.pallas_call(kernel, out_shape=[jax.ShapeDtypeStruct(s, d) for s, d in...  6.77 us
  transfers between devices with their start and end apart: 24, of which 17 were waited for; matrix products, arithmetic and copies ran while one was open for 0% of the time, Pallas kernels for 4%

profile of v1, /device:TPU:0, one launch (start us, length us, event | category | flops | bytes accessed | tf_op | source)
XLA Modules:
  0.0 81.5 jit_solution(6091829810710968057)
XLA Ops:
  0.0 3.0 %collective-permute-start.5 = (bf16[2,4,128,2,128]{4,3,2,1,0:T(2,128)(2,1)}, bf16[2,4,128,2,128]{4,3,2,1,0:T(2,128)(2,1)S(1)}, u32[]{:S(2)}, u32[]{:S(2)}) collective-permute-start(bf16[2,4,128,2,128]{4,3,2,1,0:T(2,128)(2,1)} %param.4), channel_id=1, source_target_pairs={{0,16},{1,17},{2,18},{3,19},{4,20},{5,21},{6,22},{7,23},{8,24},{9,... | collective-permute-start | bytes 1572872 | tf_op jit(solution)/shard_map/ppermute | solution.py:20
  3.0 1.5 %collective-permute-start.4 = (bf16[2,4,128,2,128]{4,3,2,1,0:T(2,128)(2,1)}, bf16[2,4,128,2,128]{4,3,2,1,0:T(2,128)(2,1)S(1)}, u32[]{:S(2)}, u32[]{:S(2)}) collective-permute-start(bf16[2,4,128,2,128]{4,3,2,1,0:T(2,128)(2,1)} %param.4), channel_id=1, source_target_pairs={{0,8},{1,9},{2,10},{3,11},{4,12},{5,13},{6,14},{7,15},{8,0},{9,1},... | collective-permute-start | bytes 1572872 | tf_op jit(solution)/shard_map/ppermute | solution.py:20
  4.5 10.6 %collective-permute-done.5.ref = bf16[2,4,128,2,128]{4,3,2,1,0:T(2,128)(2,1)S(1)} collective-permute-done((bf16[2,4,128,2,128]{4,3,2,1,0:T(2,128)(2,1)}, bf16[2,4,128,2,128]{4,3,2,1,0:T(2,128)(2,1)S(1)}, u32[]{:S(2)}, u32[]{:S(2)}) %collective-permute-start.5) | collective-permute-done | bytes 524320 | tf_op jit(solution)/shard_map/ppermute | solution.py:20
  15.1 1.8 %collective-permute-start.14 = (bf16[1,4,128,2,128]{4,3,2,1,0:T(2,128)(2,1)S(1)}, bf16[1,4,128,2,128]{4,3,2,1,0:T(2,128)(2,1)S(1)}, u32[]{:S(2)}, u32[]{:S(2)}) collective-permute-start(bf16[1,4,128,2,128]{4,3,2,1,0:T(2,128)(2,1)S(1)} %shard_map.55), channel_id=1, source_target_pairs={{0,8},{1,9},{2,10},{3,11},{4,12},{5,13},{6,14},{7,15},{8,0},{9,1},... | collective-permute-start | bytes 786440 | tf_op jit(solution)/shard_map/ppermute | solution.py:20
  17.0 1.6 %collective-permute-start.15 = (bf16[1,4,128,2,128]{4,3,2,1,0:T(2,128)(2,1)S(1)}, bf16[1,4,128,2,128]{4,3,2,1,0:T(2,128)(2,1)S(1)}, u32[]{:S(2)}, u32[]{:S(2)}) collective-permute-start(bf16[1,4,128,2,128]{4,3,2,1,0:T(2,128)(2,1)S(1)} %shard_map.56), channel_id=1, source_target_pairs={{0,16},{1,17},{2,18},{3,19},{4,20},{5,21},{6,22},{7,23},{8,24},{9,... | collective-permute-start | bytes 786440 | tf_op jit(solution)/shard_map/ppermute | solution.py:20
  20.6 2.1 %collective-permute-done.14 = bf16[1,4,128,2,128]{4,3,2,1,0:T(2,128)(2,1)S(1)} collective-permute-done((bf16[1,4,128,2,128]{4,3,2,1,0:T(2,128)(2,1)S(1)}, bf16[1,4,128,2,128]{4,3,2,1,0:T(2,128)(2,1)S(1)}, u32[]{:S(2)}, u32[]{:S(2)}) %collective-permute-start.14) | collective-permute-done | bytes 262176 | tf_op jit(solution)/shard_map/ppermute | solution.py:20
  26.1 3.6 %collective-permute-start.3 = (bf16[2,2,64,128]{3,2,1,0:T(8,128)(2,1)S(1)}, bf16[2,2,64,128]{3,2,1,0:T(8,128)(2,1)S(1)}, u32[]{:S(2)}, u32[]{:S(2)}) collective-permute-start(bf16[2,2,64,128]{3,2,1,0:T(8,128)(2,1)S(1)} %shard_map.47.refs_0_.free_ref), channel_id=1, source_target_pairs={{0,6},{1,7},{2,4},{3,5},{4,2},{5,3},{6,0},{7,1},{8,14},{9,15},{10,... | collective-permute-start | bytes 196616 | tf_op jit(solution)/shard_map/ppermute | solution.py:20
  29.7 2.5 %collective-permute-done.3.refs_3_ = bf16[2,2,64,128]{3,2,1,0:T(8,128)(2,1)S(1)} collective-permute-done((bf16[2,2,64,128]{3,2,1,0:T(8,128)(2,1)S(1)}, bf16[2,2,64,128]{3,2,1,0:T(8,128)(2,1)S(1)}, u32[]{:S(2)}, u32[]{:S(2)}) %collective-permute-start.3) | collective-permute-done | bytes 65568 | tf_op jit(solution)/shard_map/ppermute | solution.py:20
  33.0 4.4 %collective-permute-done.2.refs_2_ = bf16[2,2,64,128]{3,2,1,0:T(8,128)(2,1)S(1)} collective-permute-done((bf16[2,2,64,128]{3,2,1,0:T(8,128)(2,1)S(1)}, bf16[2,2,64,128]{3,2,1,0:T(8,128)(2,1)S(1)}, u32[]{:S(2)}, u32[]{:S(2)}) %collective-permute-start.2) | collective-permute-done | bytes 65568 | tf_op jit(solution)/shard_map/ppermute | solution.py:20
  38.7 3.0 %collective-permute-done.1.refs_1_ = bf16[2,2,64,128]{3,2,1,0:T(8,128)(2,1)S(1)} collective-permute-done((bf16[2,2,64,128]{3,2,1,0:T(8,128)(2,1)S(1)}, bf16[2,2,64,128]{3,2,1,0:T(8,128)(2,1)S(1)}, u32[]{:S(2)}, u32[]{:S(2)}) %collective-permute-start.1) | collective-permute-done | bytes 65568 | tf_op jit(solution)/shard_map/ppermute | solution.py:20
  43.6 3.2 %collective-permute-done.9.tile_ref = bf16[2,2,64,128]{3,2,1,0:T(8,128)(2,1)S(1)} collective-permute-done((bf16[2,2,64,128]{3,2,1,0:T(8,128)(2,1)S(1)}, bf16[2,2,64,128]{3,2,1,0:T(8,128)(2,1)S(1)}, u32[]{:S(2)}, u32[]{:S(2)}) %collective-permute-start.9) | collective-permute-done | bytes 65568 | tf_op jit(solution)/shard_map/ppermute | solution.py:20
  48.8 1.3 %shard_map.51.near_ref = f32[2,2,32,256]{3,2,1,0:T(8,128)S(1)} custom-call(s32[2]{0:T(128)S(1)} %copy-done.2, s32[1]{0:T(128)S(6)} %copy.5.now_ref, bf16[2,2,64,128]{3,2,1,0:T(8,128)(2,1)S(1)} %shard_map.47.refs_0_.free_ref, bf16[2,2,64,128]{3,2,1,0:T(8,128)(2,1)S(1)} %collective-permute-done.1.refs_1_, ...), custom_call_target="tpu_custom_call" | custom-call | tf_op jit(solution)/shard_map/pallas_call | solution.py:27
  50.2 1.8 %collective-permute-done.10.far_ref = bf16[2,2,32,256]{3,2,1,0:T(8,128)(2,1)S(1)} collective-permute-done((bf16[2,2,32,256]{3,2,1,0:T(8,128)(2,1)S(1)}, bf16[2,2,32,256]{3,2,1,0:T(8,128)(2,1)S(1)}, u32[]{:S(2)}, u32[]{:S(2)}) %collective-permute-start.10) | collective-permute-done | bytes 65568 | tf_op jit(solution)/shard_map/ppermute | solution.py:20
  52.0 3.2 %collective-permute-start.13 = (bf16[2,2,64,128]{3,2,1,0:T(8,128)(2,1)S(1)}, bf16[2,2,64,128]{3,2,1,0:T(8,128)(2,1)S(1)}, u32[]{:S(2)}, u32[]{:S(2)}) collective-permute-start(bf16[2,2,64,128]{3,2,1,0:T(8,128)(2,1)S(1)} %shard_map.54.refs_0_), channel_id=1, source_target_pairs={{0,6},{1,7},{2,4},{3,5},{4,2},{5,3},{6,0},{7,1},{8,14},{9,15},{10,... | collective-permute-start | bytes 196616 | tf_op jit(solution)/shard_map/ppermute | solution.py:20
  56.4 1.7 %collective-permute-done.13.refs_3_ = bf16[2,2,64,128]{3,2,1,0:T(8,128)(2,1)S(1)} collective-permute-done((bf16[2,2,64,128]{3,2,1,0:T(8,128)(2,1)S(1)}, bf16[2,2,64,128]{3,2,1,0:T(8,128)(2,1)S(1)}, u32[]{:S(2)}, u32[]{:S(2)}) %collective-permute-start.13) | collective-permute-done | bytes 65568 | tf_op jit(solution)/shard_map/ppermute | solution.py:20
  58.1 3.8 %collective-permute-done.12.refs_2_ = bf16[2,2,64,128]{3,2,1,0:T(8,128)(2,1)S(1)} collective-permute-done((bf16[2,2,64,128]{3,2,1,0:T(8,128)(2,1)S(1)}, bf16[2,2,64,128]{3,2,1,0:T(8,128)(2,1)S(1)}, u32[]{:S(2)}, u32[]{:S(2)}) %collective-permute-start.12) | collective-permute-done | bytes 65568 | tf_op jit(solution)/shard_map/ppermute | solution.py:20
  61.9 1.5 %shard_map.58.refs_0_ = bf16[2,2,64,128]{3,2,1,0:T(8,128)(2,1)S(1)} custom-call(s32[2]{0:T(128)S(1)} %copy-done.2, s32[1]{0:T(128)S(6)} %copy.5.now_ref, bf16[2,2,64,128]{3,2,1,0:T(8,128)(2,1)S(1)} %shard_map.47.refs_0_.free_ref, bf16[2,2,64,128]{3,2,1,0:T(8,128)(2,1)S(1)} %shard_map.54.refs_0_, bf16[2,2,64,128]{3,2,1,0:T(8,128)(2,1)S(1)} %collective-permute-done.11.refs_1_, ...), custom_call_target="tpu_custom_call" | custom-call | tf_op jit(solution)/shard_map/pallas_call | solution.py:27
  63.5 2.4 %collective-permute-start.19 = (bf16[2,2,64,128]{3,2,1,0:T(8,128)(2,1)S(1)}, bf16[2,2,64,128]{3,2,1,0:T(8,128)(2,1)S(1)}, u32[]{:S(2)}, u32[]{:S(2)}) collective-permute-start(bf16[2,2,64,128]{3,2,1,0:T(8,128)(2,1)S(1)} %shard_map.58.refs_0_), channel_id=1, source_target_pairs={{0,6},{1,7},{2,4},{3,5},{4,2},{5,3},{6,0},{7,1},{8,14},{9,15},{10,... | collective-permute-start | bytes 196616 | tf_op jit(solution)/shard_map/ppermute | solution.py:20
  65.9 2.1 %collective-permute-start.17 = (bf16[2,2,64,128]{3,2,1,0:T(8,128)(2,1)S(1)}, bf16[2,2,64,128]{3,2,1,0:T(8,128)(2,1)S(1)}, u32[]{:S(2)}, u32[]{:S(2)}) collective-permute-start(bf16[2,2,64,128]{3,2,1,0:T(8,128)(2,1)S(1)} %shard_map.58.refs_0_), channel_id=1, source_target_pairs={{0,2},{1,3},{2,0},{3,1},{4,6},{5,7},{6,4},{7,5},{8,10},{9,11},{10,... | collective-permute-start | bytes 196616 | tf_op jit(solution)/shard_map/ppermute | solution.py:20
  67.9 1.7 %collective-permute-done.19.refs_3_ = bf16[2,2,64,128]{3,2,1,0:T(8,128)(2,1)S(1)} collective-permute-done((bf16[2,2,64,128]{3,2,1,0:T(8,128)(2,1)S(1)}, bf16[2,2,64,128]{3,2,1,0:T(8,128)(2,1)S(1)}, u32[]{:S(2)}, u32[]{:S(2)}) %collective-permute-start.19) | collective-permute-done | bytes 65568 | tf_op jit(solution)/shard_map/ppermute | solution.py:20
  69.6 1.4 %collective-permute-done.18.refs_2_ = bf16[2,2,64,128]{3,2,1,0:T(8,128)(2,1)S(1)} collective-permute-done((bf16[2,2,64,128]{3,2,1,0:T(8,128)(2,1)S(1)}, bf16[2,2,64,128]{3,2,1,0:T(8,128)(2,1)S(1)}, u32[]{:S(2)}, u32[]{:S(2)}) %collective-permute-start.18) | collective-permute-done | bytes 65568 | tf_op jit(solution)/shard_map/ppermute | solution.py:20
  71.0 1.5 %shard_map.59 = bf16[2,2,64,128]{3,2,1,0:T(8,128)(2,1)S(1)} custom-call(s32[2]{0:T(128)S(1)} %copy-done.2, s32[1]{0:T(128)S(6)} %copy.5.now_ref, bf16[2,2,64,128]{3,2,1,0:T(8,128)(2,1)S(1)} %shard_map.47.refs_0_.free_ref, bf16[2,2,64,128]{3,2,1,0:T(8,128)(2,1)S(1)} %shard_map.58.refs_0_, bf16[2,2,64,128]{3,2,1,0:T(8,128)(2,1)S(1)} %collective-permute-done.17.refs_1_, ...), custom_call_target="tpu_custom_call" | custom-call | tf_op jit(solution)/shard_map/pallas_call | solution.py:27
  73.9 1.5 %collective-permute-start.23 = (bf16[2,2,64,128]{3,2,1,0:T(8,128)(2,1)S(1)}, bf16[2,2,64,128]{3,2,1,0:T(8,128)(2,1)S(1)}, u32[]{:S(2)}, u32[]{:S(2)}) collective-permute-start(bf16[2,2,64,128]{3,2,1,0:T(8,128)(2,1)S(1)} %shard_map.60.refs_0_), channel_id=1, source_target_pairs={{0,24},{1,25},{2,26},{3,27},{4,28},{5,29},{6,30},{7,31},{8,16},{9,... | collective-permute-start | bytes 196616 | tf_op jit(solution)/shard_map/ppermute | solution.py:20
  77.3 1.7 %collective-permute-done.23.refs_3_ = bf16[2,2,64,128]{3,2,1,0:T(8,128)(2,1)S(1)} collective-permute-done((bf16[2,2,64,128]{3,2,1,0:T(8,128)(2,1)S(1)}, bf16[2,2,64,128]{3,2,1,0:T(8,128)(2,1)S(1)}, u32[]{:S(2)}, u32[]{:S(2)}) %collective-permute-start.23) | collective-permute-done | bytes 65568 | tf_op jit(solution)/shard_map/ppermute | solution.py:20
  (47 shorter events, 17.9 us)
Async XLA Ops:
  0.0 15.1 %collective-permute-start.5 = (bf16[2,4,128,2,128]{4,3,2,1,0:T(2,128)(2,1)}, bf16[2,4,128,2,128]{4,3,2,1,0:T(2,128)(2,1)S(1)}, u32[]{:S(2)}, u32[]{:S(2)}) collective-permute-start(bf16[2,4,128,2,128]{4,3,2,1,0:T(2,128)(2,1)} %param.4), channel_id=1, source_target_pairs={{0,16},{1,17},{2,18},{3,19},{4,20},{5,21},{6,22},{7,23},{8,24},{9,... | collective-permute-start | bytes 1572872 | tf_op jit(solution)/shard_map/ppermute | solution.py:20
  3.0 13.9 %collective-permute-start.4 = (bf16[2,4,128,2,128]{4,3,2,1,0:T(2,128)(2,1)}, bf16[2,4,128,2,128]{4,3,2,1,0:T(2,128)(2,1)S(1)}, u32[]{:S(2)}, u32[]{:S(2)}) collective-permute-start(bf16[2,4,128,2,128]{4,3,2,1,0:T(2,128)(2,1)} %param.4), channel_id=1, source_target_pairs={{0,8},{1,9},{2,10},{3,11},{4,12},{5,13},{6,14},{7,15},{8,0},{9,1},... | collective-permute-start | bytes 1572872 | tf_op jit(solution)/shard_map/ppermute | solution.py:20
  15.1 7.5 %collective-permute-start.14 = (bf16[1,4,128,2,128]{4,3,2,1,0:T(2,128)(2,1)S(1)}, bf16[1,4,128,2,128]{4,3,2,1,0:T(2,128)(2,1)S(1)}, u32[]{:S(2)}, u32[]{:S(2)}) collective-permute-start(bf16[1,4,128,2,128]{4,3,2,1,0:T(2,128)(2,1)S(1)} %shard_map.55), channel_id=1, source_target_pairs={{0,8},{1,9},{2,10},{3,11},{4,12},{5,13},{6,14},{7,15},{8,0},{9,1},... | collective-permute-start | bytes 786440 | tf_op jit(solution)/shard_map/ppermute | solution.py:20
  17.0 7.0 %collective-permute-start.15 = (bf16[1,4,128,2,128]{4,3,2,1,0:T(2,128)(2,1)S(1)}, bf16[1,4,128,2,128]{4,3,2,1,0:T(2,128)(2,1)S(1)}, u32[]{:S(2)}, u32[]{:S(2)}) collective-permute-start(bf16[1,4,128,2,128]{4,3,2,1,0:T(2,128)(2,1)S(1)} %shard_map.56), channel_id=1, source_target_pairs={{0,16},{1,17},{2,18},{3,19},{4,20},{5,21},{6,22},{7,23},{8,24},{9,... | collective-permute-start | bytes 786440 | tf_op jit(solution)/shard_map/ppermute | solution.py:20
  18.7 28.0 %collective-permute-start.8 = (bf16[2,4,128,256]{3,2,1,0:T(8,128)(2,1)S(1)}, bf16[2,4,128,256]{3,2,1,0:T(8,128)(2,1)S(1)}, u32[]{:S(2)}, u32[]{:S(2)}) collective-permute-start(bf16[2,4,128,256]{3,2,1,0:T(8,128)(2,1)S(1)} %shard_map.50.refs_6_.own), channel_id=1, source_target_pairs={{0,1},{1,0},{2,3},{3,2},{4,5},{5,4},{6,7},{7,6},{8,9},{9,8},{10,11... | collective-permute-start | bytes 1572872 | tf_op jit(solution)/shard_map/ppermute | solution.py:20
  19.8 29.0 %collective-permute-start.6 = (bf16[2,4,128,256]{3,2,1,0:T(8,128)(2,1)S(1)}, bf16[2,4,128,256]{3,2,1,0:T(8,128)(2,1)S(1)}, u32[]{:S(2)}, u32[]{:S(2)}) collective-permute-start(bf16[2,4,128,256]{3,2,1,0:T(8,128)(2,1)S(1)} %shard_map.48.refs_4_), channel_id=1, source_target_pairs={{0,1},{1,0},{2,3},{3,2},{4,5},{5,4},{6,7},{7,6},{8,9},{9,8},{10,11... | collective-permute-start | bytes 1572872 | tf_op jit(solution)/shard_map/ppermute | solution.py:20
  20.0 28.8 %collective-permute-start.7 = (bf16[2,4,128,256]{3,2,1,0:T(8,128)(2,1)S(1)}, bf16[2,4,128,256]{3,2,1,0:T(8,128)(2,1)S(1)}, u32[]{:S(2)}, u32[]{:S(2)}) collective-permute-start(bf16[2,4,128,256]{3,2,1,0:T(8,128)(2,1)S(1)} %shard_map.49.refs_5_), channel_id=1, source_target_pairs={{0,1},{1,0},{2,3},{3,2},{4,5},{5,4},{6,7},{7,6},{8,9},{9,8},{10,11... | collective-permute-start | bytes 1572872 | tf_op jit(solution)/shard_map/ppermute | solution.py:20
  24.1 37.8 %collective-permute-start.16 = (bf16[2,4,128,256]{3,2,1,0:T(8,128)(2,1)S(1)}, bf16[2,4,128,256]{3,2,1,0:T(8,128)(2,1)S(1)}, u32[]{:S(2)}, u32[]{:S(2)}) collective-permute-start(bf16[2,4,128,256]{3,2,1,0:T(8,128)(2,1)S(1)} %shard_map.57.refs_7_), channel_id=1, source_target_pairs={{0,1},{1,0},{2,3},{3,2},{4,5},{5,4},{6,7},{7,6},{8,9},{9,8},{10,11... | collective-permute-start | bytes 1572872 | tf_op jit(solution)/shard_map/ppermute | solution.py:20
  24.9 1.2 %collective-permute-start = (bf16[2,64,128]{2,1,0:T(8,128)(2,1)S(1)}, bf16[2,64,128]{2,1,0:T(8,128)(2,1)S(1)}, u32[]{:S(2)}, u32[]{:S(2)}) collective-permute-start(bf16[2,64,128]{2,1,0:T(8,128)(2,1)S(1)} %bitcast.20), channel_id=1, source_target_pairs={{0,1},{1,0},{2,3},{3,2},{4,5},{5,4},{6,7},{7,6},{8,9},{9,8},{10,11... | collective-permute-start | bytes 98312 | tf_op jit(solution)/shard_map/ppermute | solution.py:20
  26.1 6.1 %collective-permute-start.3 = (bf16[2,2,64,128]{3,2,1,0:T(8,128)(2,1)S(1)}, bf16[2,2,64,128]{3,2,1,0:T(8,128)(2,1)S(1)}, u32[]{:S(2)}, u32[]{:S(2)}) collective-permute-start(bf16[2,2,64,128]{3,2,1,0:T(8,128)(2,1)S(1)} %shard_map.47.refs_0_.free_ref), channel_id=1, source_target_pairs={{0,6},{1,7},{2,4},{3,5},{4,2},{5,3},{6,0},{7,1},{8,14},{9,15},{10,... | collective-permute-start | bytes 196616 | tf_op jit(solution)/shard_map/ppermute | solution.py:20
  32.2 5.2 %collective-permute-start.2 = (bf16[2,2,64,128]{3,2,1,0:T(8,128)(2,1)S(1)}, bf16[2,2,64,128]{3,2,1,0:T(8,128)(2,1)S(1)}, u32[]{:S(2)}, u32[]{:S(2)}) collective-permute-start(bf16[2,2,64,128]{3,2,1,0:T(8,128)(2,1)S(1)} %shard_map.47.refs_0_.free_ref), channel_id=1, source_target_pairs={{0,4},{1,5},{2,6},{3,7},{4,0},{5,1},{6,2},{7,3},{8,12},{9,13},{10,... | collective-permute-start | bytes 196616 | tf_op jit(solution)/shard_map/ppermute | solution.py:20
  37.4 4.3 %collective-permute-start.1 = (bf16[2,2,64,128]{3,2,1,0:T(8,128)(2,1)S(1)}, bf16[2,2,64,128]{3,2,1,0:T(8,128)(2,1)S(1)}, u32[]{:S(2)}, u32[]{:S(2)}) collective-permute-start(bf16[2,2,64,128]{3,2,1,0:T(8,128)(2,1)S(1)} %shard_map.47.refs_0_.free_ref), channel_id=1, source_target_pairs={{0,2},{1,3},{2,0},{3,1},{4,6},{5,7},{6,4},{7,5},{8,10},{9,11},{10,... | collective-permute-start | bytes 196616 | tf_op jit(solution)/shard_map/ppermute | solution.py:20
  41.7 5.0 %collective-permute-start.9 = (bf16[2,2,64,128]{3,2,1,0:T(8,128)(2,1)S(1)}, bf16[2,2,64,128]{3,2,1,0:T(8,128)(2,1)S(1)}, u32[]{:S(2)}, u32[]{:S(2)}) collective-permute-start(bf16[2,2,64,128]{3,2,1,0:T(8,128)(2,1)S(1)} %shard_map.52), channel_id=1, source_target_pairs={{0,8},{1,9},{2,10},{3,11},{4,12},{5,13},{6,14},{7,15},{8,0},{9,1},... | collective-permute-start | bytes 196616 | tf_op jit(solution)/shard_map/ppermute | solution.py:20
  47.6 4.3 %collective-permute-start.10 = (bf16[2,2,32,256]{3,2,1,0:T(8,128)(2,1)S(1)}, bf16[2,2,32,256]{3,2,1,0:T(8,128)(2,1)S(1)}, u32[]{:S(2)}, u32[]{:S(2)}) collective-permute-start(bf16[2,2,32,256]{3,2,1,0:T(8,128)(2,1)S(1)} %shard_map.53), channel_id=1, source_target_pairs={{0,8},{1,9},{2,10},{3,11},{4,12},{5,13},{6,14},{7,15},{8,0},{9,1},... | collective-permute-start | bytes 196616 | tf_op jit(solution)/shard_map/ppermute | solution.py:20
  52.0 6.1 %collective-permute-start.13 = (bf16[2,2,64,128]{3,2,1,0:T(8,128)(2,1)S(1)}, bf16[2,2,64,128]{3,2,1,0:T(8,128)(2,1)S(1)}, u32[]{:S(2)}, u32[]{:S(2)}) collective-permute-start(bf16[2,2,64,128]{3,2,1,0:T(8,128)(2,1)S(1)} %shard_map.54.refs_0_), channel_id=1, source_target_pairs={{0,6},{1,7},{2,4},{3,5},{4,2},{5,3},{6,0},{7,1},{8,14},{9,15},{10,... | collective-permute-start | bytes 196616 | tf_op jit(solution)/shard_map/ppermute | solution.py:20
  55.1 6.8 %collective-permute-start.12 = (bf16[2,2,64,128]{3,2,1,0:T(8,128)(2,1)S(1)}, bf16[2,2,64,128]{3,2,1,0:T(8,128)(2,1)S(1)}, u32[]{:S(2)}, u32[]{:S(2)}) collective-permute-start(bf16[2,2,64,128]{3,2,1,0:T(8,128)(2,1)S(1)} %shard_map.54.refs_0_), channel_id=1, source_target_pairs={{0,4},{1,5},{2,6},{3,7},{4,0},{5,1},{6,2},{7,3},{8,12},{9,13},{10,... | collective-permute-start | bytes 196616 | tf_op jit(solution)/shard_map/ppermute | solution.py:20
  55.1 6.8 %collective-permute-start.11 = (bf16[2,2,64,128]{3,2,1,0:T(8,128)(2,1)S(1)}, bf16[2,2,64,128]{3,2,1,0:T(8,128)(2,1)S(1)}, u32[]{:S(2)}, u32[]{:S(2)}) collective-permute-start(bf16[2,2,64,128]{3,2,1,0:T(8,128)(2,1)S(1)} %shard_map.54.refs_0_), channel_id=1, source_target_pairs={{0,2},{1,3},{2,0},{3,1},{4,6},{5,7},{6,4},{7,5},{8,10},{9,11},{10,... | collective-permute-start | bytes 196616 | tf_op jit(solution)/shard_map/ppermute | solution.py:20
  63.5 6.1 %collective-permute-start.19 = (bf16[2,2,64,128]{3,2,1,0:T(8,128)(2,1)S(1)}, bf16[2,2,64,128]{3,2,1,0:T(8,128)(2,1)S(1)}, u32[]{:S(2)}, u32[]{:S(2)}) collective-permute-start(bf16[2,2,64,128]{3,2,1,0:T(8,128)(2,1)S(1)} %shard_map.58.refs_0_), channel_id=1, source_target_pairs={{0,6},{1,7},{2,4},{3,5},{4,2},{5,3},{6,0},{7,1},{8,14},{9,15},{10,... | collective-permute-start | bytes 196616 | tf_op jit(solution)/shard_map/ppermute | solution.py:20
  65.9 5.2 %collective-permute-start.18 = (bf16[2,2,64,128]{3,2,1,0:T(8,128)(2,1)S(1)}, bf16[2,2,64,128]{3,2,1,0:T(8,128)(2,1)S(1)}, u32[]{:S(2)}, u32[]{:S(2)}) collective-permute-start(bf16[2,2,64,128]{3,2,1,0:T(8,128)(2,1)S(1)} %shard_map.58.refs_0_), channel_id=1, source_target_pairs={{0,4},{1,5},{2,6},{3,7},{4,0},{5,1},{6,2},{7,3},{8,12},{9,13},{10,... | collective-permute-start | bytes 196616 | tf_op jit(solution)/shard_map/ppermute | solution.py:20
  65.9 5.2 %collective-permute-start.17 = (bf16[2,2,64,128]{3,2,1,0:T(8,128)(2,1)S(1)}, bf16[2,2,64,128]{3,2,1,0:T(8,128)(2,1)S(1)}, u32[]{:S(2)}, u32[]{:S(2)}) collective-permute-start(bf16[2,2,64,128]{3,2,1,0:T(8,128)(2,1)S(1)} %shard_map.58.refs_0_), channel_id=1, source_target_pairs={{0,2},{1,3},{2,0},{3,1},{4,6},{5,7},{6,4},{7,5},{8,10},{9,11},{10,... | collective-permute-start | bytes 196616 | tf_op jit(solution)/shard_map/ppermute | solution.py:20
  72.6 1.3 %collective-permute-start.20 = (bf16[2,64,128]{2,1,0:T(8,128)(2,1)S(1)}, bf16[2,64,128]{2,1,0:T(8,128)(2,1)S(1)}, u32[]{:S(2)}, u32[]{:S(2)}) collective-permute-start(bf16[2,64,128]{2,1,0:T(8,128)(2,1)S(1)} %get-tuple-element.9), channel_id=1, source_target_pairs={{0,1},{1,0},{2,3},{3,2},{4,5},{5,4},{6,7},{7,6},{8,9},{9,8},{10,11... | collective-permute-start | bytes 98312 | tf_op jit(solution)/shard_map/ppermute | solution.py:20
  73.9 5.2 %collective-permute-start.23 = (bf16[2,2,64,128]{3,2,1,0:T(8,128)(2,1)S(1)}, bf16[2,2,64,128]{3,2,1,0:T(8,128)(2,1)S(1)}, u32[]{:S(2)}, u32[]{:S(2)}) collective-permute-start(bf16[2,2,64,128]{3,2,1,0:T(8,128)(2,1)S(1)} %shard_map.60.refs_0_), channel_id=1, source_target_pairs={{0,24},{1,25},{2,26},{3,27},{4,28},{5,29},{6,30},{7,31},{8,16},{9,... | collective-permute-start | bytes 196616 | tf_op jit(solution)/shard_map/ppermute | solution.py:20
  75.3 5.0 %collective-permute-start.22 = (bf16[2,2,64,128]{3,2,1,0:T(8,128)(2,1)S(1)}, bf16[2,2,64,128]{3,2,1,0:T(8,128)(2,1)S(1)}, u32[]{:S(2)}, u32[]{:S(2)}) collective-permute-start(bf16[2,2,64,128]{3,2,1,0:T(8,128)(2,1)S(1)} %shard_map.60.refs_0_), channel_id=1, source_target_pairs={{0,16},{1,17},{2,18},{3,19},{4,20},{5,21},{6,22},{7,23},{8,24},{9,... | collective-permute-start | bytes 196616 | tf_op jit(solution)/shard_map/ppermute | solution.py:20
  76.5 4.3 %collective-permute-start.21 = (bf16[2,2,64,128]{3,2,1,0:T(8,128)(2,1)S(1)}, bf16[2,2,64,128]{3,2,1,0:T(8,128)(2,1)S(1)}, u32[]{:S(2)}, u32[]{:S(2)}) collective-permute-start(bf16[2,2,64,128]{3,2,1,0:T(8,128)(2,1)S(1)} %shard_map.60.refs_0_), channel_id=1, source_target_pairs={{0,8},{1,9},{2,10},{3,11},{4,12},{5,13},{6,14},{7,15},{8,0},{9,1},... | collective-permute-start | bytes 196616 | tf_op jit(solution)/shard_map/ppermute | solution.py:20
  (3 other events, 7.0 us)

commit v2 on v1

--- a/solution.py
+++ b/solution.py
@@ -78,18 +78,24 @@
     )
 
 
-def put_sigma(tile, b, dims, start_ref, now_ref, wide, sig):
-    row_count, orb_rows, cols, lanes = dims
-    rows = row_count * orb_rows
-    row_of = lax.broadcasted_iota(jnp.int32, (rows, lanes), 0) // orb_rows
-    for p in range(2):
-        wide[p] = tile[p].astype(jnp.float32)
-    for c in range(cols):
-        s = b * cols + c
+def live_kernel(row_count, start_ref, now_ref, out_ref):
+    times, rows, lanes = out_ref.shape
+    row_of = lax.broadcasted_iota(jnp.int32, (rows, lanes), 0) // (rows // row_count)
+    for s in range(times):
         weight = jnp.zeros((rows, lanes), jnp.float32)
         for r in range(row_count):
             on = (s >= start_ref[r]) & (s < now_ref[0] + r)
             weight = jnp.where(row_of == r, jnp.where(on, 1.0, 0.0), weight)
+        out_ref[s] = weight
+
+
+def put_sigma(tile, b, dims, live_ref, wide, sig):
+    row_count, orb_rows, cols, lanes = dims
+    rows = row_count * orb_rows
+    for p in range(2):
+        wide[p] = tile[p].astype(jnp.float32)
+    for c in range(cols):
+        weight = live_ref[b * cols + c]
         real = wide[0, pl.ds(c, rows, stride=cols), :]
         imag = wide[1, pl.ds(c, rows, stride=cols), :]
         modulus = real * real + imag * imag
@@ -120,9 +126,9 @@
     return free.astype(jnp.float32) + COUPLING * wide[p]
 
 
-def integral(tiles, hists, masks, dims, start_ref, now_ref, wide, sig):
+def integral(tiles, hists, masks, dims, live_ref, wide, sig):
     for k, (tile, block, place) in enumerate(tiles):
-        put_sigma(tile, block, dims, start_ref, now_ref, wide.at[k], sig.at[place])
+        put_sigma(tile, block, dims, live_ref, wide.at[k], sig.at[place])
     zero = jnp.zeros((2 * dims[0] * dims[1], dims[2] * dims[3]), jnp.float32)
     sums = [(zero, zero), (zero, zero)]
     for i, mask in enumerate(masks):
@@ -138,19 +144,19 @@
     return [(block.at[e], tt ^ (2 * k + e), tt ^ (2 * k + e)) for k, block in enumerate(blocks) for e in range(2)]
 
 
-def help_kernel(dims, lent, start_ref, now_ref, tile_ref, own, pair, out_ref, wide, sig):
+def help_kernel(dims, lent, live_ref, tile_ref, own, pair, out_ref, wide, sig):
     core = lax.axis_index("tt") % 2
     block = lax.axis_index("mem") ^ lent
     tiles = [(tile_ref.at[e], block * 2 + (core ^ e), core ^ e) for e in range(2)]
-    for e, value in enumerate(integral(tiles, (own, pair), (0,), dims, start_ref, now_ref, wide, sig)):
+    for e, value in enumerate(integral(tiles, (own, pair), (0,), dims, live_ref, wide, sig)):
         for p in range(2):
             out_ref[e, p] = value[p].astype(out_ref.dtype)
 
 
-def near_kernel(dims, count, near, start_ref, now_ref, *refs):
+def near_kernel(dims, count, near, live_ref, *refs):
     blocks, hists, (out_ref, wide, sig) = refs[:count], refs[count:-3], refs[-3:]
     masks = [lax.axis_index("mem") ^ q for q in near]
-    for e, value in enumerate(integral(all_tiles(blocks), hists, masks, dims, start_ref, now_ref, wide, sig)):
+    for e, value in enumerate(integral(all_tiles(blocks), hists, masks, dims, live_ref, wide, sig)):
         for p in range(2):
             out_ref[e, p] = value[p]
 
@@ -163,10 +169,10 @@
             out_ref[e, p] = update(free_ref[e, p], value, dims, wide.at[e], p).astype(out_ref.dtype)
 
 
-def step_kernel(dims, count, n_mem, start_ref, now_ref, free_ref, *refs):
+def step_kernel(dims, count, n_mem, live_ref, free_ref, *refs):
     blocks, hists, (out_ref, wide, sig) = refs[:count], refs[count:-3], refs[-3:]
     masks = [lax.axis_index("mem") ^ q for q in range(n_mem)]
-    for e, value in enumerate(integral(all_tiles(blocks), hists, masks, dims, start_ref, now_ref, wide, sig)):
+    for e, value in enumerate(integral(all_tiles(blocks), hists, masks, dims, live_ref, wide, sig)):
         for p in range(2):
             out_ref[e, p] = update(free_ref[e, p], value[p], dims, wide.at[e], p).astype(out_ref.dtype)
 
@@ -195,9 +201,9 @@
     if n_tt != 2 * n_mem:
         raise ValueError("unequal split")
     parts, row_count, orb_count, cols, lanes = free_rows.shape
+    spans = history.shape[1]
     orb_rows = orb_count // n_mem
     bf16, f32 = jnp.bfloat16, jnp.float32
-    live = (memory_start, now)
     dims = (row_count, orb_rows // 2, cols, lanes)
     rows = row_count * orb_rows // 2
     size = orb_rows * cols // 2
@@ -243,6 +249,9 @@
     keep, give = (a.reshape(parts, rows * cols, lanes) for a in (keep, give))
     free = stack(keep, swap(give, 0, 1))
     blocks = gather_current(free)
+    live = call(
+        functools.partial(live_kernel, row_count), ((spans * n_mem, rows, lanes), f32), [memory_start, now], smem=2
+    )
 
     last, helper = n_mem - 1, 1
     lent = last ^ helper
@@ -256,17 +265,15 @@
     lent_sum = call(
         functools.partial(help_kernel, dims, lent),
         ((2, parts, rows, cols * lanes), bf16),
-        [*live, lent_block, split[lent], pair[lent]],
+        [live, lent_block, split[lent], pair[lent]],
         scratch(2),
-        smem=2,
     )
     last_sum = swap(lent_sum, helper, 0)
     near_sum = call(
         functools.partial(near_kernel, dims, len(blocks), near),
         ((2, parts, rows, cols * lanes), f32),
-        [*live, *blocks, *(split[q] for q in near), *(pair[q] for q in near)],
+        [live, *blocks, *(split[q] for q in near), *(pair[q] for q in near)],
         scratch(n_tt),
-        smem=2,
     )
     current = call(
         functools.partial(first_kernel, dims),
@@ -282,9 +289,8 @@
         current = call(
             functools.partial(step_kernel, dims, len(blocks), n_mem),
             (free.shape, bf16),
-            [*live, free, *blocks, *hists],
+            [live, free, *blocks, *hists],
             scratch(n_tt),
-            smem=2,
         )
         if sweep < ITERS - 1:
             blocks = gather_current(current)

time: 81.7 us -> 80.1 us (0.980)
  Pallas kernels: 6.77 us -> 5.16 us
    pallas_call x16 -> x17, Pallas kernels: 6.77 us -> 5.16 us  [call(): pl.pallas_call(kernel, out_shape=[jax.ShapeDtypeStruct(s, d) for s, d in...]
  transfers between devices with their start and end apart: 24 -> 24, of which waited for: 17 -> 17; matrix products, arithmetic and copies ran while one was open for 0% -> 0% of each run, Pallas kernels for 4% -> 3%
where the time goes in v2:
time: 80.1 us; the launch traced here: 79.9 us
  waiting for transfers between devices  43 us (54%)
  starting transfers between devices  29.4 us (37%)
  Pallas kernels  5.16 us (6%)
  local copies, waits for them, and re-layouts  1.48 us (2%)
    ppermute x24, waiting for transfers between devices, swap(): return lax.ppermute(value, BOTH, pairs)  43 us
    ppermute x24, starting transfers between devices, swap(): return lax.ppermute(value, BOTH, pairs)  29.4 us
    pallas_call x17, Pallas kernels, call(): pl.pallas_call(kernel, out_shape=[jax.ShapeDtypeStruct(s, d) for s, d in...  5.16 us
  transfers between devices with their start and end apart: 24, of which 17 were waited for; matrix products, arithmetic and copies ran while one was open for 0% of the time, Pallas kernels for 3%

profile of v2, /device:TPU:0, one launch (start us, length us, event | category | flops | bytes accessed | tf_op | source)
XLA Modules:
  0.0 79.9 jit_solution(9152211294389164798)
XLA Ops:
  0.0 3.0 %collective-permute-start.5 = (bf16[2,4,128,2,128]{4,3,2,1,0:T(2,128)(2,1)}, bf16[2,4,128,2,128]{4,3,2,1,0:T(2,128)(2,1)S(1)}, u32[]{:S(2)}, u32[]{:S(2)}) collective-permute-start(bf16[2,4,128,2,128]{4,3,2,1,0:T(2,128)(2,1)} %param.4), channel_id=1, source_target_pairs={{0,16},{1,17},{2,18},{3,19},{4,20},{5,21},{6,22},{7,23},{8,24},{9,... | collective-permute-start | bytes 1572872 | tf_op jit(solution)/shard_map/ppermute | solution.py:20
  3.0 1.5 %collective-permute-start.4 = (bf16[2,4,128,2,128]{4,3,2,1,0:T(2,128)(2,1)}, bf16[2,4,128,2,128]{4,3,2,1,0:T(2,128)(2,1)S(1)}, u32[]{:S(2)}, u32[]{:S(2)}) collective-permute-start(bf16[2,4,128,2,128]{4,3,2,1,0:T(2,128)(2,1)} %param.4), channel_id=1, source_target_pairs={{0,8},{1,9},{2,10},{3,11},{4,12},{5,13},{6,14},{7,15},{8,0},{9,1},... | collective-permute-start | bytes 1572872 | tf_op jit(solution)/shard_map/ppermute | solution.py:20
  4.5 10.6 %collective-permute-done.5.ref = bf16[2,4,128,2,128]{4,3,2,1,0:T(2,128)(2,1)S(1)} collective-permute-done((bf16[2,4,128,2,128]{4,3,2,1,0:T(2,128)(2,1)}, bf16[2,4,128,2,128]{4,3,2,1,0:T(2,128)(2,1)S(1)}, u32[]{:S(2)}, u32[]{:S(2)}) %collective-permute-start.5) | collective-permute-done | bytes 524320 | tf_op jit(solution)/shard_map/ppermute | solution.py:20
  15.1 1.8 %collective-permute-start.14 = (bf16[1,4,128,2,128]{4,3,2,1,0:T(2,128)(2,1)S(1)}, bf16[1,4,128,2,128]{4,3,2,1,0:T(2,128)(2,1)S(1)}, u32[]{:S(2)}, u32[]{:S(2)}) collective-permute-start(bf16[1,4,128,2,128]{4,3,2,1,0:T(2,128)(2,1)S(1)} %shard_map.56), channel_id=1, source_target_pairs={{0,8},{1,9},{2,10},{3,11},{4,12},{5,13},{6,14},{7,15},{8,0},{9,1},... | collective-permute-start | bytes 786440 | tf_op jit(solution)/shard_map/ppermute | solution.py:20
  17.0 1.6 %collective-permute-start.15 = (bf16[1,4,128,2,128]{4,3,2,1,0:T(2,128)(2,1)S(1)}, bf16[1,4,128,2,128]{4,3,2,1,0:T(2,128)(2,1)S(1)}, u32[]{:S(2)}, u32[]{:S(2)}) collective-permute-start(bf16[1,4,128,2,128]{4,3,2,1,0:T(2,128)(2,1)S(1)} %shard_map.57), channel_id=1, source_target_pairs={{0,16},{1,17},{2,18},{3,19},{4,20},{5,21},{6,22},{7,23},{8,24},{9,... | collective-permute-start | bytes 786440 | tf_op jit(solution)/shard_map/ppermute | solution.py:20
  20.6 2.1 %collective-permute-done.14 = bf16[1,4,128,2,128]{4,3,2,1,0:T(2,128)(2,1)S(1)} collective-permute-done((bf16[1,4,128,2,128]{4,3,2,1,0:T(2,128)(2,1)S(1)}, bf16[1,4,128,2,128]{4,3,2,1,0:T(2,128)(2,1)S(1)}, u32[]{:S(2)}, u32[]{:S(2)}) %collective-permute-start.14) | collective-permute-done | bytes 262176 | tf_op jit(solution)/shard_map/ppermute | solution.py:20
  22.7 1.2 %collective-permute-done.15 = bf16[1,4,128,2,128]{4,3,2,1,0:T(2,128)(2,1)S(1)} collective-permute-done((bf16[1,4,128,2,128]{4,3,2,1,0:T(2,128)(2,1)S(1)}, bf16[1,4,128,2,128]{4,3,2,1,0:T(2,128)(2,1)S(1)}, u32[]{:S(2)}, u32[]{:S(2)}) %collective-permute-start.15) | collective-permute-done | bytes 262176 | tf_op jit(solution)/shard_map/ppermute | solution.py:20
  24.9 1.2 %collective-permute-done.b_ref = bf16[2,64,128]{2,1,0:T(8,128)(2,1)S(1)} collective-permute-done((bf16[2,64,128]{2,1,0:T(8,128)(2,1)S(1)}, bf16[2,64,128]{2,1,0:T(8,128)(2,1)S(1)}, u32[]{:S(2)}, u32[]{:S(2)}) %collective-permute-start) | collective-permute-done | bytes 32800 | tf_op jit(solution)/shard_map/ppermute | solution.py:20
  26.1 3.6 %collective-permute-start.3 = (bf16[2,2,64,128]{3,2,1,0:T(8,128)(2,1)S(1)}, bf16[2,2,64,128]{3,2,1,0:T(8,128)(2,1)S(1)}, u32[]{:S(2)}, u32[]{:S(2)}) collective-permute-start(bf16[2,2,64,128]{3,2,1,0:T(8,128)(2,1)S(1)} %shard_map.48.refs_0_.free_ref), channel_id=1, source_target_pairs={{0,6},{1,7},{2,4},{3,5},{4,2},{5,3},{6,0},{7,1},{8,14},{9,15},{10,... | collective-permute-start | bytes 196616 | tf_op jit(solution)/shard_map/ppermute | solution.py:20
  29.7 2.5 %collective-permute-done.3.refs_3_ = bf16[2,2,64,128]{3,2,1,0:T(8,128)(2,1)S(1)} collective-permute-done((bf16[2,2,64,128]{3,2,1,0:T(8,128)(2,1)S(1)}, bf16[2,2,64,128]{3,2,1,0:T(8,128)(2,1)S(1)}, u32[]{:S(2)}, u32[]{:S(2)}) %collective-permute-start.3) | collective-permute-done | bytes 65568 | tf_op jit(solution)/shard_map/ppermute | solution.py:20
  33.0 4.4 %collective-permute-done.2.refs_2_ = bf16[2,2,64,128]{3,2,1,0:T(8,128)(2,1)S(1)} collective-permute-done((bf16[2,2,64,128]{3,2,1,0:T(8,128)(2,1)S(1)}, bf16[2,2,64,128]{3,2,1,0:T(8,128)(2,1)S(1)}, u32[]{:S(2)}, u32[]{:S(2)}) %collective-permute-start.2) | collective-permute-done | bytes 65568 | tf_op jit(solution)/shard_map/ppermute | solution.py:20
  37.4 1.3 %collective-permute-start.1 = (bf16[2,2,64,128]{3,2,1,0:T(8,128)(2,1)S(1)}, bf16[2,2,64,128]{3,2,1,0:T(8,128)(2,1)S(1)}, u32[]{:S(2)}, u32[]{:S(2)}) collective-permute-start(bf16[2,2,64,128]{3,2,1,0:T(8,128)(2,1)S(1)} %shard_map.48.refs_0_.free_ref), channel_id=1, source_target_pairs={{0,2},{1,3},{2,0},{3,1},{4,6},{5,7},{6,4},{7,5},{8,10},{9,11},{10,... | collective-permute-start | bytes 196616 | tf_op jit(solution)/shard_map/ppermute | solution.py:20
  38.7 3.0 %collective-permute-done.1.refs_1_ = bf16[2,2,64,128]{3,2,1,0:T(8,128)(2,1)S(1)} collective-permute-done((bf16[2,2,64,128]{3,2,1,0:T(8,128)(2,1)S(1)}, bf16[2,2,64,128]{3,2,1,0:T(8,128)(2,1)S(1)}, u32[]{:S(2)}, u32[]{:S(2)}) %collective-permute-start.1) | collective-permute-done | bytes 65568 | tf_op jit(solution)/shard_map/ppermute | solution.py:20
  44.2 2.0 %collective-permute-done.9.tile_ref = bf16[2,2,64,128]{3,2,1,0:T(8,128)(2,1)S(1)} collective-permute-done((bf16[2,2,64,128]{3,2,1,0:T(8,128)(2,1)S(1)}, bf16[2,2,64,128]{3,2,1,0:T(8,128)(2,1)S(1)}, u32[]{:S(2)}, u32[]{:S(2)}) %collective-permute-start.9) | collective-permute-done | bytes 65568 | tf_op jit(solution)/shard_map/ppermute | solution.py:20
  46.5 1.2 %collective-permute-start.10 = (bf16[2,2,32,256]{3,2,1,0:T(8,128)(2,1)S(1)}, bf16[2,2,32,256]{3,2,1,0:T(8,128)(2,1)S(1)}, u32[]{:S(2)}, u32[]{:S(2)}) collective-permute-start(bf16[2,2,32,256]{3,2,1,0:T(8,128)(2,1)S(1)} %shard_map.54), channel_id=1, source_target_pairs={{0,8},{1,9},{2,10},{3,11},{4,12},{5,13},{6,14},{7,15},{8,0},{9,1},... | collective-permute-start | bytes 196616 | tf_op jit(solution)/shard_map/ppermute | solution.py:20
  48.5 2.3 %collective-permute-done.10.far_ref = bf16[2,2,32,256]{3,2,1,0:T(8,128)(2,1)S(1)} collective-permute-done((bf16[2,2,32,256]{3,2,1,0:T(8,128)(2,1)S(1)}, bf16[2,2,32,256]{3,2,1,0:T(8,128)(2,1)S(1)}, u32[]{:S(2)}, u32[]{:S(2)}) %collective-permute-start.10) | collective-permute-done | bytes 65568 | tf_op jit(solution)/shard_map/ppermute | solution.py:20
  50.9 4.1 %collective-permute-start.13 = (bf16[2,2,64,128]{3,2,1,0:T(8,128)(2,1)S(1)}, bf16[2,2,64,128]{3,2,1,0:T(8,128)(2,1)S(1)}, u32[]{:S(2)}, u32[]{:S(2)}) collective-permute-start(bf16[2,2,64,128]{3,2,1,0:T(8,128)(2,1)S(1)} %shard_map.55.refs_0_), channel_id=1, source_target_pairs={{0,6},{1,7},{2,4},{3,5},{4,2},{5,3},{6,0},{7,1},{8,14},{9,15},{10,... | collective-permute-start | bytes 196616 | tf_op jit(solution)/shard_map/ppermute | solution.py:20
  55.6 1.6 %collective-permute-done.13.refs_3_ = bf16[2,2,64,128]{3,2,1,0:T(8,128)(2,1)S(1)} collective-permute-done((bf16[2,2,64,128]{3,2,1,0:T(8,128)(2,1)S(1)}, bf16[2,2,64,128]{3,2,1,0:T(8,128)(2,1)S(1)}, u32[]{:S(2)}, u32[]{:S(2)}) %collective-permute-start.13) | collective-permute-done | bytes 65568 | tf_op jit(solution)/shard_map/ppermute | solution.py:20
  57.2 4.8 %collective-permute-done.12.refs_2_ = bf16[2,2,64,128]{3,2,1,0:T(8,128)(2,1)S(1)} collective-permute-done((bf16[2,2,64,128]{3,2,1,0:T(8,128)(2,1)S(1)}, bf16[2,2,64,128]{3,2,1,0:T(8,128)(2,1)S(1)}, u32[]{:S(2)}, u32[]{:S(2)}) %collective-permute-start.12) | collective-permute-done | bytes 65568 | tf_op jit(solution)/shard_map/ppermute | solution.py:20
  64.2 3.3 %collective-permute-start.17 = (bf16[2,2,64,128]{3,2,1,0:T(8,128)(2,1)S(1)}, bf16[2,2,64,128]{3,2,1,0:T(8,128)(2,1)S(1)}, u32[]{:S(2)}, u32[]{:S(2)}) collective-permute-start(bf16[2,2,64,128]{3,2,1,0:T(8,128)(2,1)S(1)} %shard_map.59.refs_0_), channel_id=1, source_target_pairs={{0,2},{1,3},{2,0},{3,1},{4,6},{5,7},{6,4},{7,5},{8,10},{9,11},{10,... | collective-permute-start | bytes 196616 | tf_op jit(solution)/shard_map/ppermute | solution.py:20
  67.5 1.8 %collective-permute-done.19.refs_3_ = bf16[2,2,64,128]{3,2,1,0:T(8,128)(2,1)S(1)} collective-permute-done((bf16[2,2,64,128]{3,2,1,0:T(8,128)(2,1)S(1)}, bf16[2,2,64,128]{3,2,1,0:T(8,128)(2,1)S(1)}, u32[]{:S(2)}, u32[]{:S(2)}) %collective-permute-start.19) | collective-permute-done | bytes 65568 | tf_op jit(solution)/shard_map/ppermute | solution.py:20
  72.3 1.5 %collective-permute-start.23 = (bf16[2,2,64,128]{3,2,1,0:T(8,128)(2,1)S(1)}, bf16[2,2,64,128]{3,2,1,0:T(8,128)(2,1)S(1)}, u32[]{:S(2)}, u32[]{:S(2)}) collective-permute-start(bf16[2,2,64,128]{3,2,1,0:T(8,128)(2,1)S(1)} %shard_map.61.refs_0_), channel_id=1, source_target_pairs={{0,24},{1,25},{2,26},{3,27},{4,28},{5,29},{6,30},{7,31},{8,16},{9,... | collective-permute-start | bytes 196616 | tf_op jit(solution)/shard_map/ppermute | solution.py:20
  75.8 1.7 %collective-permute-done.23.refs_3_ = bf16[2,2,64,128]{3,2,1,0:T(8,128)(2,1)S(1)} collective-permute-done((bf16[2,2,64,128]{3,2,1,0:T(8,128)(2,1)S(1)}, bf16[2,2,64,128]{3,2,1,0:T(8,128)(2,1)S(1)}, u32[]{:S(2)}, u32[]{:S(2)}) %collective-permute-start.23) | collective-permute-done | bytes 65568 | tf_op jit(solution)/shard_map/ppermute | solution.py:20
  77.4 1.3 %collective-permute-done.22.refs_2_ = bf16[2,2,64,128]{3,2,1,0:T(8,128)(2,1)S(1)} collective-permute-done((bf16[2,2,64,128]{3,2,1,0:T(8,128)(2,1)S(1)}, bf16[2,2,64,128]{3,2,1,0:T(8,128)(2,1)S(1)}, u32[]{:S(2)}, u32[]{:S(2)}) %collective-permute-start.22) | collective-permute-done | bytes 65568 | tf_op jit(solution)/shard_map/ppermute | solution.py:20
  (48 shorter events, 15.6 us)
Async XLA Ops:
  0.0 15.1 %collective-permute-start.5 = (bf16[2,4,128,2,128]{4,3,2,1,0:T(2,128)(2,1)}, bf16[2,4,128,2,128]{4,3,2,1,0:T(2,128)(2,1)S(1)}, u32[]{:S(2)}, u32[]{:S(2)}) collective-permute-start(bf16[2,4,128,2,128]{4,3,2,1,0:T(2,128)(2,1)} %param.4), channel_id=1, source_target_pairs={{0,16},{1,17},{2,18},{3,19},{4,20},{5,21},{6,22},{7,23},{8,24},{9,... | collective-permute-start | bytes 1572872 | tf_op jit(solution)/shard_map/ppermute | solution.py:20
  3.0 13.9 %collective-permute-start.4 = (bf16[2,4,128,2,128]{4,3,2,1,0:T(2,128)(2,1)}, bf16[2,4,128,2,128]{4,3,2,1,0:T(2,128)(2,1)S(1)}, u32[]{:S(2)}, u32[]{:S(2)}) collective-permute-start(bf16[2,4,128,2,128]{4,3,2,1,0:T(2,128)(2,1)} %param.4), channel_id=1, source_target_pairs={{0,8},{1,9},{2,10},{3,11},{4,12},{5,13},{6,14},{7,15},{8,0},{9,1},... | collective-permute-start | bytes 1572872 | tf_op jit(solution)/shard_map/ppermute | solution.py:20
  15.1 7.5 %collective-permute-start.14 = (bf16[1,4,128,2,128]{4,3,2,1,0:T(2,128)(2,1)S(1)}, bf16[1,4,128,2,128]{4,3,2,1,0:T(2,128)(2,1)S(1)}, u32[]{:S(2)}, u32[]{:S(2)}) collective-permute-start(bf16[1,4,128,2,128]{4,3,2,1,0:T(2,128)(2,1)S(1)} %shard_map.56), channel_id=1, source_target_pairs={{0,8},{1,9},{2,10},{3,11},{4,12},{5,13},{6,14},{7,15},{8,0},{9,1},... | collective-permute-start | bytes 786440 | tf_op jit(solution)/shard_map/ppermute | solution.py:20
  17.0 7.0 %collective-permute-start.15 = (bf16[1,4,128,2,128]{4,3,2,1,0:T(2,128)(2,1)S(1)}, bf16[1,4,128,2,128]{4,3,2,1,0:T(2,128)(2,1)S(1)}, u32[]{:S(2)}, u32[]{:S(2)}) collective-permute-start(bf16[1,4,128,2,128]{4,3,2,1,0:T(2,128)(2,1)S(1)} %shard_map.57), channel_id=1, source_target_pairs={{0,16},{1,17},{2,18},{3,19},{4,20},{5,21},{6,22},{7,23},{8,24},{9,... | collective-permute-start | bytes 786440 | tf_op jit(solution)/shard_map/ppermute | solution.py:20
  18.7 27.5 %collective-permute-start.8 = (bf16[2,4,128,256]{3,2,1,0:T(8,128)(2,1)S(1)}, bf16[2,4,128,256]{3,2,1,0:T(8,128)(2,1)S(1)}, u32[]{:S(2)}, u32[]{:S(2)}) collective-permute-start(bf16[2,4,128,256]{3,2,1,0:T(8,128)(2,1)S(1)} %shard_map.51.refs_6_.own), channel_id=1, source_target_pairs={{0,1},{1,0},{2,3},{3,2},{4,5},{5,4},{6,7},{7,6},{8,9},{9,8},{10,11... | collective-permute-start | bytes 1572872 | tf_op jit(solution)/shard_map/ppermute | solution.py:20
  19.8 28.0 %collective-permute-start.6 = (bf16[2,4,128,256]{3,2,1,0:T(8,128)(2,1)S(1)}, bf16[2,4,128,256]{3,2,1,0:T(8,128)(2,1)S(1)}, u32[]{:S(2)}, u32[]{:S(2)}) collective-permute-start(bf16[2,4,128,256]{3,2,1,0:T(8,128)(2,1)S(1)} %shard_map.49.refs_4_), channel_id=1, source_target_pairs={{0,1},{1,0},{2,3},{3,2},{4,5},{5,4},{6,7},{7,6},{8,9},{9,8},{10,11... | collective-permute-start | bytes 1572872 | tf_op jit(solution)/shard_map/ppermute | solution.py:20
  20.0 27.7 %collective-permute-start.7 = (bf16[2,4,128,256]{3,2,1,0:T(8,128)(2,1)S(1)}, bf16[2,4,128,256]{3,2,1,0:T(8,128)(2,1)S(1)}, u32[]{:S(2)}, u32[]{:S(2)}) collective-permute-start(bf16[2,4,128,256]{3,2,1,0:T(8,128)(2,1)S(1)} %shard_map.50.refs_5_), channel_id=1, source_target_pairs={{0,1},{1,0},{2,3},{3,2},{4,5},{5,4},{6,7},{7,6},{8,9},{9,8},{10,11... | collective-permute-start | bytes 1572872 | tf_op jit(solution)/shard_map/ppermute | solution.py:20
  24.1 37.9 %collective-permute-start.16 = (bf16[2,4,128,256]{3,2,1,0:T(8,128)(2,1)S(1)}, bf16[2,4,128,256]{3,2,1,0:T(8,128)(2,1)S(1)}, u32[]{:S(2)}, u32[]{:S(2)}) collective-permute-start(bf16[2,4,128,256]{3,2,1,0:T(8,128)(2,1)S(1)} %shard_map.58.refs_7_), channel_id=1, source_target_pairs={{0,1},{1,0},{2,3},{3,2},{4,5},{5,4},{6,7},{7,6},{8,9},{9,8},{10,11... | collective-permute-start | bytes 1572872 | tf_op jit(solution)/shard_map/ppermute | solution.py:20
  24.9 1.2 %collective-permute-start = (bf16[2,64,128]{2,1,0:T(8,128)(2,1)S(1)}, bf16[2,64,128]{2,1,0:T(8,128)(2,1)S(1)}, u32[]{:S(2)}, u32[]{:S(2)}) collective-permute-start(bf16[2,64,128]{2,1,0:T(8,128)(2,1)S(1)} %bitcast.20), channel_id=1, source_target_pairs={{0,1},{1,0},{2,3},{3,2},{4,5},{5,4},{6,7},{7,6},{8,9},{9,8},{10,11... | collective-permute-start | bytes 98312 | tf_op jit(solution)/shard_map/ppermute | solution.py:20
  26.1 6.1 %collective-permute-start.3 = (bf16[2,2,64,128]{3,2,1,0:T(8,128)(2,1)S(1)}, bf16[2,2,64,128]{3,2,1,0:T(8,128)(2,1)S(1)}, u32[]{:S(2)}, u32[]{:S(2)}) collective-permute-start(bf16[2,2,64,128]{3,2,1,0:T(8,128)(2,1)S(1)} %shard_map.48.refs_0_.free_ref), channel_id=1, source_target_pairs={{0,6},{1,7},{2,4},{3,5},{4,2},{5,3},{6,0},{7,1},{8,14},{9,15},{10,... | collective-permute-start | bytes 196616 | tf_op jit(solution)/shard_map/ppermute | solution.py:20
  32.2 5.2 %collective-permute-start.2 = (bf16[2,2,64,128]{3,2,1,0:T(8,128)(2,1)S(1)}, bf16[2,2,64,128]{3,2,1,0:T(8,128)(2,1)S(1)}, u32[]{:S(2)}, u32[]{:S(2)}) collective-permute-start(bf16[2,2,64,128]{3,2,1,0:T(8,128)(2,1)S(1)} %shard_map.48.refs_0_.free_ref), channel_id=1, source_target_pairs={{0,4},{1,5},{2,6},{3,7},{4,0},{5,1},{6,2},{7,3},{8,12},{9,13},{10,... | collective-permute-start | bytes 196616 | tf_op jit(solution)/shard_map/ppermute | solution.py:20
  37.4 4.3 %collective-permute-start.1 = (bf16[2,2,64,128]{3,2,1,0:T(8,128)(2,1)S(1)}, bf16[2,2,64,128]{3,2,1,0:T(8,128)(2,1)S(1)}, u32[]{:S(2)}, u32[]{:S(2)}) collective-permute-start(bf16[2,2,64,128]{3,2,1,0:T(8,128)(2,1)S(1)} %shard_map.48.refs_0_.free_ref), channel_id=1, source_target_pairs={{0,2},{1,3},{2,0},{3,1},{4,6},{5,7},{6,4},{7,5},{8,10},{9,11},{10,... | collective-permute-start | bytes 196616 | tf_op jit(solution)/shard_map/ppermute | solution.py:20
  41.7 4.5 %collective-permute-start.9 = (bf16[2,2,64,128]{3,2,1,0:T(8,128)(2,1)S(1)}, bf16[2,2,64,128]{3,2,1,0:T(8,128)(2,1)S(1)}, u32[]{:S(2)}, u32[]{:S(2)}) collective-permute-start(bf16[2,2,64,128]{3,2,1,0:T(8,128)(2,1)S(1)} %shard_map.53), channel_id=1, source_target_pairs={{0,8},{1,9},{2,10},{3,11},{4,12},{5,13},{6,14},{7,15},{8,0},{9,1},... | collective-permute-start | bytes 196616 | tf_op jit(solution)/shard_map/ppermute | solution.py:20
  46.5 4.3 %collective-permute-start.10 = (bf16[2,2,32,256]{3,2,1,0:T(8,128)(2,1)S(1)}, bf16[2,2,32,256]{3,2,1,0:T(8,128)(2,1)S(1)}, u32[]{:S(2)}, u32[]{:S(2)}) collective-permute-start(bf16[2,2,32,256]{3,2,1,0:T(8,128)(2,1)S(1)} %shard_map.54), channel_id=1, source_target_pairs={{0,8},{1,9},{2,10},{3,11},{4,12},{5,13},{6,14},{7,15},{8,0},{9,1},... | collective-permute-start | bytes 196616 | tf_op jit(solution)/shard_map/ppermute | solution.py:20
  50.9 6.3 %collective-permute-start.13 = (bf16[2,2,64,128]{3,2,1,0:T(8,128)(2,1)S(1)}, bf16[2,2,64,128]{3,2,1,0:T(8,128)(2,1)S(1)}, u32[]{:S(2)}, u32[]{:S(2)}) collective-permute-start(bf16[2,2,64,128]{3,2,1,0:T(8,128)(2,1)S(1)} %shard_map.55.refs_0_), channel_id=1, source_target_pairs={{0,6},{1,7},{2,4},{3,5},{4,2},{5,3},{6,0},{7,1},{8,14},{9,15},{10,... | collective-permute-start | bytes 196616 | tf_op jit(solution)/shard_map/ppermute | solution.py:20
  55.0 7.1 %collective-permute-start.12 = (bf16[2,2,64,128]{3,2,1,0:T(8,128)(2,1)S(1)}, bf16[2,2,64,128]{3,2,1,0:T(8,128)(2,1)S(1)}, u32[]{:S(2)}, u32[]{:S(2)}) collective-permute-start(bf16[2,2,64,128]{3,2,1,0:T(8,128)(2,1)S(1)} %shard_map.55.refs_0_), channel_id=1, source_target_pairs={{0,4},{1,5},{2,6},{3,7},{4,0},{5,1},{6,2},{7,3},{8,12},{9,13},{10,... | collective-permute-start | bytes 196616 | tf_op jit(solution)/shard_map/ppermute | solution.py:20
  55.0 7.1 %collective-permute-start.11 = (bf16[2,2,64,128]{3,2,1,0:T(8,128)(2,1)S(1)}, bf16[2,2,64,128]{3,2,1,0:T(8,128)(2,1)S(1)}, u32[]{:S(2)}, u32[]{:S(2)}) collective-permute-start(bf16[2,2,64,128]{3,2,1,0:T(8,128)(2,1)S(1)} %shard_map.55.refs_0_), channel_id=1, source_target_pairs={{0,2},{1,3},{2,0},{3,1},{4,6},{5,7},{6,4},{7,5},{8,10},{9,11},{10,... | collective-permute-start | bytes 196616 | tf_op jit(solution)/shard_map/ppermute | solution.py:20
  63.0 6.3 %collective-permute-start.19 = (bf16[2,2,64,128]{3,2,1,0:T(8,128)(2,1)S(1)}, bf16[2,2,64,128]{3,2,1,0:T(8,128)(2,1)S(1)}, u32[]{:S(2)}, u32[]{:S(2)}) collective-permute-start(bf16[2,2,64,128]{3,2,1,0:T(8,128)(2,1)S(1)} %shard_map.59.refs_0_), channel_id=1, source_target_pairs={{0,6},{1,7},{2,4},{3,5},{4,2},{5,3},{6,0},{7,1},{8,14},{9,15},{10,... | collective-permute-start | bytes 196616 | tf_op jit(solution)/shard_map/ppermute | solution.py:20
  63.4 6.6 %collective-permute-start.18 = (bf16[2,2,64,128]{3,2,1,0:T(8,128)(2,1)S(1)}, bf16[2,2,64,128]{3,2,1,0:T(8,128)(2,1)S(1)}, u32[]{:S(2)}, u32[]{:S(2)}) collective-permute-start(bf16[2,2,64,128]{3,2,1,0:T(8,128)(2,1)S(1)} %shard_map.59.refs_0_), channel_id=1, source_target_pairs={{0,4},{1,5},{2,6},{3,7},{4,0},{5,1},{6,2},{7,3},{8,12},{9,13},{10,... | collective-permute-start | bytes 196616 | tf_op jit(solution)/shard_map/ppermute | solution.py:20
  64.2 5.8 %collective-permute-start.17 = (bf16[2,2,64,128]{3,2,1,0:T(8,128)(2,1)S(1)}, bf16[2,2,64,128]{3,2,1,0:T(8,128)(2,1)S(1)}, u32[]{:S(2)}, u32[]{:S(2)}) collective-permute-start(bf16[2,2,64,128]{3,2,1,0:T(8,128)(2,1)S(1)} %shard_map.59.refs_0_), channel_id=1, source_target_pairs={{0,2},{1,3},{2,0},{3,1},{4,6},{5,7},{6,4},{7,5},{8,10},{9,11},{10,... | collective-permute-start | bytes 196616 | tf_op jit(solution)/shard_map/ppermute | solution.py:20
  71.0 1.3 %collective-permute-start.20 = (bf16[2,64,128]{2,1,0:T(8,128)(2,1)S(1)}, bf16[2,64,128]{2,1,0:T(8,128)(2,1)S(1)}, u32[]{:S(2)}, u32[]{:S(2)}) collective-permute-start(bf16[2,64,128]{2,1,0:T(8,128)(2,1)S(1)} %get-tuple-element.9), channel_id=1, source_target_pairs={{0,1},{1,0},{2,3},{3,2},{4,5},{5,4},{6,7},{7,6},{8,9},{9,8},{10,11... | collective-permute-start | bytes 98312 | tf_op jit(solution)/shard_map/ppermute | solution.py:20
  72.3 5.2 %collective-permute-start.23 = (bf16[2,2,64,128]{3,2,1,0:T(8,128)(2,1)S(1)}, bf16[2,2,64,128]{3,2,1,0:T(8,128)(2,1)S(1)}, u32[]{:S(2)}, u32[]{:S(2)}) collective-permute-start(bf16[2,2,64,128]{3,2,1,0:T(8,128)(2,1)S(1)} %shard_map.61.refs_0_), channel_id=1, source_target_pairs={{0,24},{1,25},{2,26},{3,27},{4,28},{5,29},{6,30},{7,31},{8,16},{9,... | collective-permute-start | bytes 196616 | tf_op jit(solution)/shard_map/ppermute | solution.py:20
  73.8 5.0 %collective-permute-start.22 = (bf16[2,2,64,128]{3,2,1,0:T(8,128)(2,1)S(1)}, bf16[2,2,64,128]{3,2,1,0:T(8,128)(2,1)S(1)}, u32[]{:S(2)}, u32[]{:S(2)}) collective-permute-start(bf16[2,2,64,128]{3,2,1,0:T(8,128)(2,1)S(1)} %shard_map.61.refs_0_), channel_id=1, source_target_pairs={{0,16},{1,17},{2,18},{3,19},{4,20},{5,21},{6,22},{7,23},{8,24},{9,... | collective-permute-start | bytes 196616 | tf_op jit(solution)/shard_map/ppermute | solution.py:20
  74.9 4.3 %collective-permute-start.21 = (bf16[2,2,64,128]{3,2,1,0:T(8,128)(2,1)S(1)}, bf16[2,2,64,128]{3,2,1,0:T(8,128)(2,1)S(1)}, u32[]{:S(2)}, u32[]{:S(2)}) collective-permute-start(bf16[2,2,64,128]{3,2,1,0:T(8,128)(2,1)S(1)} %shard_map.61.refs_0_), channel_id=1, source_target_pairs={{0,8},{1,9},{2,10},{3,11},{4,12},{5,13},{6,14},{7,15},{8,0},{9,1},... | collective-permute-start | bytes 196616 | tf_op jit(solution)/shard_map/ppermute | solution.py:20
  (3 other events, 3.9 us)

commit v3 on v2

--- a/solution.py
+++ b/solution.py
@@ -10,7 +10,7 @@
 
 ITERS = 3
 COUPLING = 0.5
-VMEM_LIMIT = 20 << 20
+VMEM_LIMIT = 40 << 20
 BOTH = ("mem", "tt")
 
 
@@ -32,14 +32,6 @@
         scratch_shapes=list(scratch),
         compiler_params=pltpu.CompilerParams(vmem_limit_bytes=VMEM_LIMIT),
     )(*args)
-
-
-def rows_kernel(free_ref, keep_ref, give_ref):
-    mem, core = lax.axis_index("mem"), lax.axis_index("tt") % 2
-    for p in range(free_ref.shape[0]):
-        for r in range(free_ref.shape[1]):
-            keep_ref[p, r] = free_ref[p, r, mem, core]
-            give_ref[p, r] = free_ref[p, r, mem, 1 - core]
 
 
 def stack_kernel(a_ref, b_ref, out_ref):
@@ -177,6 +169,54 @@
             out_ref[e, p] = update(free_ref[e, p], value[p], dims, wide.at[e], p).astype(out_ref.dtype)
 
 
+def collect_kernel(*refs):
+    hists, out_ref = refs[:-1], refs[-1]
+    count = len(hists) // 2
+    for e in range(2):
+        for k in range(count):
+            out_ref[e, lax.axis_index("mem") ^ k] = hists[e * count + k][...]
+
+
+def block_integral(sums, block, k, pairs, dims, live_ref, hist_ref, wide, sig):
+    tt = lax.axis_index("tt")
+    chip, core = (tt // 2) ^ k, tt % 2
+    cols = dims[2]
+    for e in range(2):
+        h = core ^ e
+        put_sigma(block.at[e], 2 * chip + h, dims, live_ref, wide.at[2 * k + e], sig.at[2 * k + e])
+        for i, pair in enumerate(pairs):
+            at = pl.ds(h * cols, cols)
+            sums[i] = tuple(
+                total
+                + jnp.dot(
+                    sig[2 * k + e],
+                    hist_ref[pair, chip, p, at].reshape(cols * dims[3], cols * dims[3]),
+                    preferred_element_type=jnp.float32,
+                )
+                for p, total in enumerate(sums[i])
+            )
+    return sums
+
+
+def early_kernel(dims, early, live_ref, hist_ref, *refs):
+    blocks, (out_ref, wide, sig) = refs[:-3], refs[-3:]
+    zero = jnp.zeros((2 * dims[0] * dims[1], dims[2] * dims[3]), jnp.float32)
+    sums = [(zero, zero), (zero, zero)]
+    for k, block in zip(early, blocks):
+        sums = block_integral(sums, block, k, (0, 1), dims, live_ref, hist_ref, wide, sig)
+    for e in range(2):
+        for p, value in enumerate(as_complex(sums[e])):
+            out_ref[e, p] = value
+
+
+def late_kernel(dims, late, pair, live_ref, hist_ref, block, sum_ref, free_ref, out_ref, wide, sig):
+    zero = jnp.zeros((2 * dims[0] * dims[1], dims[2] * dims[3]), jnp.float32)
+    (sums,) = block_integral([(zero, zero)], block, late, (pair,), dims, live_ref, hist_ref, wide, sig)
+    for p, value in enumerate(as_complex(sums)):
+        new = update(free_ref[pair, p], sum_ref[pair, p] + value, dims, wide.at[0], p)
+        out_ref[p] = new.astype(out_ref.dtype)
+
+
 def pick_kernel(wanted, *refs):
     blocks, out_ref = refs[:-1], refs[-1]
     for k, block in enumerate(blocks):
@@ -241,10 +281,11 @@
     def parts_of(k):
         return (raw[k],) if k in raw else (part(k, 0), part(k, 1))
 
-    keep, give = call(
-        rows_kernel,
-        [((parts, row_count, size, lanes), bf16)] * 2,
-        [free_rows.reshape(parts, row_count, n_mem, 2, size, lanes)],
+    mem, core = lax.axis_index("mem"), lax.axis_index("tt") % 2
+    by_core = free_rows.reshape(parts, row_count, n_mem, 2, size, lanes)
+    keep, give = (
+        lax.dynamic_slice(by_core, (0, 0, mem, c, 0, 0), (parts, row_count, 1, 1, size, lanes))
+        for c in (core, 1 - core)
     )
     keep, give = (a.reshape(parts, rows * cols, lanes) for a in (keep, give))
     free = stack(keep, swap(give, 0, 1))
@@ -285,16 +326,34 @@
     split[last] = split_history(parts_of(last))
     pair[last] = swap(split[last], 0, 1)
     hists = [split[k] for k in range(n_mem)] + [pair[k] for k in range(n_mem)]
-    for sweep in range(1, ITERS):
+    for _ in range(1, ITERS - 1):
         current = call(
             functools.partial(step_kernel, dims, len(blocks), n_mem),
             (free.shape, bf16),
             [live, free, *blocks, *hists],
             scratch(n_tt),
         )
-        if sweep < ITERS - 1:
-            blocks = gather_current(current)
-    own = stack(current[0], swap(current[1], 0, 1))
+        blocks = gather_current(current)
+    late = n_tt // 4
+    early = tuple(k for k in range(n_tt // 2) if k != late)
+    ordered = call(collect_kernel, ((2, n_mem, *hists[0].shape), bf16), hists)
+    early_sum = call(
+        functools.partial(early_kernel, dims, early),
+        ((2, parts, rows, cols * lanes), f32),
+        [live, ordered, *(blocks[k] for k in early)],
+        scratch(n_tt),
+    )
+    final = {}
+    for e in (1, 0):
+        final[e] = call(
+            functools.partial(late_kernel, dims, late, e),
+            (free.shape[1:], bf16),
+            [live, ordered, blocks[late], early_sum, free],
+            scratch(n_tt),
+        )
+        if e:
+            swapped = swap(final[e], 0, 1)
+    own = stack(final[0], swapped)
     others = [None] * n_mem
     for k in reversed(range(1, n_mem)):
         others[k] = swap(own, k, 0)

time: 80.1 us -> 82.2 us (1.026)
  Pallas kernels: 5.16 us -> 7.36 us
    pallas_call x17 -> x19, Pallas kernels: 5.16 us -> 7.36 us  [call(): pl.pallas_call(kernel, out_shape=[jax.ShapeDtypeStruct(s, d) for s, d in...]
    ppermute x24, starting transfers between devices: 29.4 us -> 28.6 us  [swap(): return lax.ppermute(value, BOTH, pairs)]
  transfers between devices with their start and end apart: 24 -> 24, of which waited for: 17 -> 17; matrix products, arithmetic and copies ran while one was open for 0% -> 1% of each run, Pallas kernels for 3% -> 7%
where the time goes in v3:
time: 82.2 us; the launch traced here: 81.9 us
  waiting for transfers between devices  43.4 us (53%)
  starting transfers between devices  28.6 us (35%)
  Pallas kernels  7.36 us (9%)
  local copies, waits for them, and re-layouts  1.84 us (2%)
    ppermute x24, waiting for transfers between devices, swap(): return lax.ppermute(value, BOTH, pairs)  43.4 us
    ppermute x24, starting transfers between devices, swap(): return lax.ppermute(value, BOTH, pairs)  28.6 us
    pallas_call x19, Pallas kernels, call(): pl.pallas_call(kernel, out_shape=[jax.ShapeDtypeStruct(s, d) for s, d in...  7.36 us
  transfers between devices with their start and end apart: 24, of which 17 were waited for; matrix products, arithmetic and copies ran while one was open for 1% of the time, Pallas kernels for 7%

profile of v3, /device:TPU:0, one launch (start us, length us, event | category | flops | bytes accessed | tf_op | source)
XLA Modules:
  0.0 81.9 jit_solution(6520796538224519757)
XLA Ops:
  0.0 3.0 %collective-permute-start.1 = (bf16[2,4,128,2,128]{4,3,2,1,0:T(2,128)(2,1)}, bf16[2,4,128,2,128]{4,3,2,1,0:T(2,128)(2,1)S(1)}, u32[]{:S(2)}, u32[]{:S(2)}) collective-permute-start(bf16[2,4,128,2,128]{4,3,2,1,0:T(2,128)(2,1)} %param.4), channel_id=1, source_target_pairs={{0,16},{1,17},{2,18},{3,19},{4,20},{5,21},{6,22},{7,23},{8,24},{9,... | collective-permute-start | bytes 1572872 | tf_op jit(solution)/shard_map/ppermute | solution.py:20
  3.0 1.5 %collective-permute-start = (bf16[2,4,128,2,128]{4,3,2,1,0:T(2,128)(2,1)}, bf16[2,4,128,2,128]{4,3,2,1,0:T(2,128)(2,1)S(1)}, u32[]{:S(2)}, u32[]{:S(2)}) collective-permute-start(bf16[2,4,128,2,128]{4,3,2,1,0:T(2,128)(2,1)} %param.4), channel_id=1, source_target_pairs={{0,8},{1,9},{2,10},{3,11},{4,12},{5,13},{6,14},{7,15},{8,0},{9,1},... | collective-permute-start | bytes 1572872 | tf_op jit(solution)/shard_map/ppermute | solution.py:20
  4.5 10.6 %collective-permute-done.1.ref = bf16[2,4,128,2,128]{4,3,2,1,0:T(2,128)(2,1)S(1)} collective-permute-done((bf16[2,4,128,2,128]{4,3,2,1,0:T(2,128)(2,1)}, bf16[2,4,128,2,128]{4,3,2,1,0:T(2,128)(2,1)S(1)}, u32[]{:S(2)}, u32[]{:S(2)}) %collective-permute-start.1) | collective-permute-done | bytes 524320 | tf_op jit(solution)/shard_map/ppermute | solution.py:20
  15.2 1.8 %collective-permute-start.2 = (bf16[1,4,128,2,128]{4,3,2,1,0:T(2,128)(2,1)S(1)}, bf16[1,4,128,2,128]{4,3,2,1,0:T(2,128)(2,1)}, u32[]{:S(2)}, u32[]{:S(2)}) collective-permute-start(bf16[1,4,128,2,128]{4,3,2,1,0:T(2,128)(2,1)S(1)} %shard_map.50), channel_id=1, source_target_pairs={{0,8},{1,9},{2,10},{3,11},{4,12},{5,13},{6,14},{7,15},{8,0},{9,1},... | collective-permute-start | bytes 786440 | tf_op jit(solution)/shard_map/ppermute | solution.py:20
  17.7 1.5 %collective-permute-start.3 = (bf16[1,4,128,2,128]{4,3,2,1,0:T(2,128)(2,1)}, bf16[1,4,128,2,128]{4,3,2,1,0:T(2,128)(2,1)}, u32[]{:S(2)}, u32[]{:S(2)}) collective-permute-start(bf16[1,4,128,2,128]{4,3,2,1,0:T(2,128)(2,1)} %shard_map.51), channel_id=1, source_target_pairs={{0,16},{1,17},{2,18},{3,19},{4,20},{5,21},{6,22},{7,23},{8,24},{9,... | collective-permute-start | bytes 786440 | tf_op jit(solution)/shard_map/ppermute | solution.py:20
  21.5 1.3 %collective-permute-done.2 = bf16[1,4,128,2,128]{4,3,2,1,0:T(2,128)(2,1)} collective-permute-done((bf16[1,4,128,2,128]{4,3,2,1,0:T(2,128)(2,1)S(1)}, bf16[1,4,128,2,128]{4,3,2,1,0:T(2,128)(2,1)}, u32[]{:S(2)}, u32[]{:S(2)}) %collective-permute-start.2) | collective-permute-done | bytes 262176 | tf_op jit(solution)/shard_map/ppermute | solution.py:20
  22.8 2.1 %collective-permute-done.3 = bf16[1,4,128,2,128]{4,3,2,1,0:T(2,128)(2,1)} collective-permute-done((bf16[1,4,128,2,128]{4,3,2,1,0:T(2,128)(2,1)}, bf16[1,4,128,2,128]{4,3,2,1,0:T(2,128)(2,1)}, u32[]{:S(2)}, u32[]{:S(2)}) %collective-permute-start.3) | collective-permute-done | bytes 262176 | tf_op jit(solution)/shard_map/ppermute | solution.py:20
  28.3 3.6 %collective-permute-start.11 = (bf16[2,2,64,128]{3,2,1,0:T(8,128)(2,1)S(1)}, bf16[2,2,64,128]{3,2,1,0:T(8,128)(2,1)S(1)}, u32[]{:S(2)}, u32[]{:S(2)}) collective-permute-start(bf16[2,2,64,128]{3,2,1,0:T(8,128)(2,1)S(1)} %shard_map.54.refs_0_.free_ref), channel_id=1, source_target_pairs={{0,6},{1,7},{2,4},{3,5},{4,2},{5,3},{6,0},{7,1},{8,14},{9,15},{10,... | collective-permute-start | bytes 196616 | tf_op jit(solution)/shard_map/ppermute | solution.py:20
  31.9 2.7 %collective-permute-done.11.refs_3_ = bf16[2,2,64,128]{3,2,1,0:T(8,128)(2,1)S(1)} collective-permute-done((bf16[2,2,64,128]{3,2,1,0:T(8,128)(2,1)S(1)}, bf16[2,2,64,128]{3,2,1,0:T(8,128)(2,1)S(1)}, u32[]{:S(2)}, u32[]{:S(2)}) %collective-permute-start.11) | collective-permute-done | bytes 65568 | tf_op jit(solution)/shard_map/ppermute | solution.py:20
  35.3 5.3 %collective-permute-done.10.refs_2_ = bf16[2,2,64,128]{3,2,1,0:T(8,128)(2,1)S(1)} collective-permute-done((bf16[2,2,64,128]{3,2,1,0:T(8,128)(2,1)S(1)}, bf16[2,2,64,128]{3,2,1,0:T(8,128)(2,1)S(1)}, u32[]{:S(2)}, u32[]{:S(2)}) %collective-permute-start.10) | collective-permute-done | bytes 65568 | tf_op jit(solution)/shard_map/ppermute | solution.py:20
  41.0 3.8 %collective-permute-done.9.refs_1_ = bf16[2,2,64,128]{3,2,1,0:T(8,128)(2,1)S(1)} collective-permute-done((bf16[2,2,64,128]{3,2,1,0:T(8,128)(2,1)S(1)}, bf16[2,2,64,128]{3,2,1,0:T(8,128)(2,1)S(1)}, u32[]{:S(2)}, u32[]{:S(2)}) %collective-permute-start.9) | collective-permute-done | bytes 65568 | tf_op jit(solution)/shard_map/ppermute | solution.py:20
  47.2 1.9 %collective-permute-done.12.tile_ref = bf16[2,2,64,128]{3,2,1,0:T(8,128)(2,1)S(1)} collective-permute-done((bf16[2,2,64,128]{3,2,1,0:T(8,128)(2,1)S(1)}, bf16[2,2,64,128]{3,2,1,0:T(8,128)(2,1)S(1)}, u32[]{:S(2)}, u32[]{:S(2)}) %collective-permute-start.12) | collective-permute-done | bytes 65568 | tf_op jit(solution)/shard_map/ppermute | solution.py:20
  49.4 1.2 %collective-permute-start.13 = (bf16[2,2,32,256]{3,2,1,0:T(8,128)(2,1)S(1)}, bf16[2,2,32,256]{3,2,1,0:T(8,128)(2,1)S(1)}, u32[]{:S(2)}, u32[]{:S(2)}) collective-permute-start(bf16[2,2,32,256]{3,2,1,0:T(8,128)(2,1)S(1)} %shard_map.57), channel_id=1, source_target_pairs={{0,8},{1,9},{2,10},{3,11},{4,12},{5,13},{6,14},{7,15},{8,0},{9,1},... | collective-permute-start | bytes 196616 | tf_op jit(solution)/shard_map/ppermute | solution.py:20
  51.4 2.3 %collective-permute-done.13.far_ref = bf16[2,2,32,256]{3,2,1,0:T(8,128)(2,1)S(1)} collective-permute-done((bf16[2,2,32,256]{3,2,1,0:T(8,128)(2,1)S(1)}, bf16[2,2,32,256]{3,2,1,0:T(8,128)(2,1)S(1)}, u32[]{:S(2)}, u32[]{:S(2)}) %collective-permute-start.13) | collective-permute-done | bytes 65568 | tf_op jit(solution)/shard_map/ppermute | solution.py:20
  53.7 3.5 %collective-permute-start.16 = (bf16[2,2,64,128]{3,2,1,0:T(8,128)(2,1)S(1)}, bf16[2,2,64,128]{3,2,1,0:T(8,128)(2,1)S(1)}, u32[]{:S(2)}, u32[]{:S(2)}) collective-permute-start(bf16[2,2,64,128]{3,2,1,0:T(8,128)(2,1)S(1)} %shard_map.58.refs_0_), channel_id=1, source_target_pairs={{0,6},{1,7},{2,4},{3,5},{4,2},{5,3},{6,0},{7,1},{8,14},{9,15},{10,... | collective-permute-start | bytes 196616 | tf_op jit(solution)/shard_map/ppermute | solution.py:20
  58.2 1.7 %collective-permute-done.16.refs_3_ = bf16[2,2,64,128]{3,2,1,0:T(8,128)(2,1)S(1)} collective-permute-done((bf16[2,2,64,128]{3,2,1,0:T(8,128)(2,1)S(1)}, bf16[2,2,64,128]{3,2,1,0:T(8,128)(2,1)S(1)}, u32[]{:S(2)}, u32[]{:S(2)}) %collective-permute-start.16) | collective-permute-done | bytes 65568 | tf_op jit(solution)/shard_map/ppermute | solution.py:20
  59.9 3.7 %collective-permute-done.15.refs_2_ = bf16[2,2,64,128]{3,2,1,0:T(8,128)(2,1)S(1)} collective-permute-done((bf16[2,2,64,128]{3,2,1,0:T(8,128)(2,1)S(1)}, bf16[2,2,64,128]{3,2,1,0:T(8,128)(2,1)S(1)}, u32[]{:S(2)}, u32[]{:S(2)}) %collective-permute-start.15) | collective-permute-done | bytes 65568 | tf_op jit(solution)/shard_map/ppermute | solution.py:20
  64.6 1.8 %collective-permute-start.19 = (bf16[2,2,64,128]{3,2,1,0:T(8,128)(2,1)S(1)}, bf16[2,2,64,128]{3,2,1,0:T(8,128)(2,1)S(1)}, u32[]{:S(2)}, u32[]{:S(2)}) collective-permute-start(bf16[2,2,64,128]{3,2,1,0:T(8,128)(2,1)S(1)} %shard_map.59.refs_0_), channel_id=1, source_target_pairs={{0,6},{1,7},{2,4},{3,5},{4,2},{5,3},{6,0},{7,1},{8,14},{9,15},{10,... | collective-permute-start | bytes 196616 | tf_op jit(solution)/shard_map/ppermute | solution.py:20
  66.4 2.6 %collective-permute-start.17 = (bf16[2,2,64,128]{3,2,1,0:T(8,128)(2,1)S(1)}, bf16[2,2,64,128]{3,2,1,0:T(8,128)(2,1)S(1)}, u32[]{:S(2)}, u32[]{:S(2)}) collective-permute-start(bf16[2,2,64,128]{3,2,1,0:T(8,128)(2,1)S(1)} %shard_map.59.refs_0_), channel_id=1, source_target_pairs={{0,4},{1,5},{2,6},{3,7},{4,0},{5,1},{6,2},{7,3},{8,12},{9,13},{10,... | collective-permute-start | bytes 196616 | tf_op jit(solution)/shard_map/ppermute | solution.py:20
  69.3 1.5 %collective-permute-done.19.refs_2_ = bf16[2,2,64,128]{3,2,1,0:T(8,128)(2,1)S(1)} collective-permute-done((bf16[2,2,64,128]{3,2,1,0:T(8,128)(2,1)S(1)}, bf16[2,2,64,128]{3,2,1,0:T(8,128)(2,1)S(1)}, u32[]{:S(2)}, u32[]{:S(2)}) %collective-permute-start.19) | collective-permute-done | bytes 65568 | tf_op jit(solution)/shard_map/ppermute | solution.py:20
  70.8 1.3 %collective-permute-done.18.refs_1_ = bf16[2,2,64,128]{3,2,1,0:T(8,128)(2,1)S(1)} collective-permute-done((bf16[2,2,64,128]{3,2,1,0:T(8,128)(2,1)S(1)}, bf16[2,2,64,128]{3,2,1,0:T(8,128)(2,1)S(1)}, u32[]{:S(2)}, u32[]{:S(2)}) %collective-permute-start.18) | collective-permute-done | bytes 65568 | tf_op jit(solution)/shard_map/ppermute | solution.py:20
  74.3 1.5 %collective-permute-start.23 = (bf16[2,2,64,128]{3,2,1,0:T(8,128)(2,1)S(1)}, bf16[2,2,64,128]{3,2,1,0:T(8,128)(2,1)S(1)}, u32[]{:S(2)}, u32[]{:S(2)}) collective-permute-start(bf16[2,2,64,128]{3,2,1,0:T(8,128)(2,1)S(1)} %shard_map.63.refs_0_), channel_id=1, source_target_pairs={{0,24},{1,25},{2,26},{3,27},{4,28},{5,29},{6,30},{7,31},{8,16},{9,... | collective-permute-start | bytes 196616 | tf_op jit(solution)/shard_map/ppermute | solution.py:20
  77.8 1.7 %collective-permute-done.23.refs_3_ = bf16[2,2,64,128]{3,2,1,0:T(8,128)(2,1)S(1)} collective-permute-done((bf16[2,2,64,128]{3,2,1,0:T(8,128)(2,1)S(1)}, bf16[2,2,64,128]{3,2,1,0:T(8,128)(2,1)S(1)}, u32[]{:S(2)}, u32[]{:S(2)}) %collective-permute-start.23) | collective-permute-done | bytes 65568 | tf_op jit(solution)/shard_map/ppermute | solution.py:20
  79.5 1.3 %collective-permute-done.22.refs_2_ = bf16[2,2,64,128]{3,2,1,0:T(8,128)(2,1)S(1)} collective-permute-done((bf16[2,2,64,128]{3,2,1,0:T(8,128)(2,1)S(1)}, bf16[2,2,64,128]{3,2,1,0:T(8,128)(2,1)S(1)}, u32[]{:S(2)}, u32[]{:S(2)}) %collective-permute-start.22) | collective-permute-done | bytes 65568 | tf_op jit(solution)/shard_map/ppermute | solution.py:20
  (48 shorter events, 18.0 us)
Async XLA Ops:
  0.0 15.1 %collective-permute-start.1 = (bf16[2,4,128,2,128]{4,3,2,1,0:T(2,128)(2,1)}, bf16[2,4,128,2,128]{4,3,2,1,0:T(2,128)(2,1)S(1)}, u32[]{:S(2)}, u32[]{:S(2)}) collective-permute-start(bf16[2,4,128,2,128]{4,3,2,1,0:T(2,128)(2,1)} %param.4), channel_id=1, source_target_pairs={{0,16},{1,17},{2,18},{3,19},{4,20},{5,21},{6,22},{7,23},{8,24},{9,... | collective-permute-start | bytes 1572872 | tf_op jit(solution)/shard_map/ppermute | solution.py:20
  3.0 13.9 %collective-permute-start = (bf16[2,4,128,2,128]{4,3,2,1,0:T(2,128)(2,1)}, bf16[2,4,128,2,128]{4,3,2,1,0:T(2,128)(2,1)S(1)}, u32[]{:S(2)}, u32[]{:S(2)}) collective-permute-start(bf16[2,4,128,2,128]{4,3,2,1,0:T(2,128)(2,1)} %param.4), channel_id=1, source_target_pairs={{0,8},{1,9},{2,10},{3,11},{4,12},{5,13},{6,14},{7,15},{8,0},{9,1},... | collective-permute-start | bytes 1572872 | tf_op jit(solution)/shard_map/ppermute | solution.py:20
  15.2 7.6 %collective-permute-start.2 = (bf16[1,4,128,2,128]{4,3,2,1,0:T(2,128)(2,1)S(1)}, bf16[1,4,128,2,128]{4,3,2,1,0:T(2,128)(2,1)}, u32[]{:S(2)}, u32[]{:S(2)}) collective-permute-start(bf16[1,4,128,2,128]{4,3,2,1,0:T(2,128)(2,1)S(1)} %shard_map.50), channel_id=1, source_target_pairs={{0,8},{1,9},{2,10},{3,11},{4,12},{5,13},{6,14},{7,15},{8,0},{9,1},... | collective-permute-start | bytes 786440 | tf_op jit(solution)/shard_map/ppermute | solution.py:20
  17.7 7.2 %collective-permute-start.3 = (bf16[1,4,128,2,128]{4,3,2,1,0:T(2,128)(2,1)}, bf16[1,4,128,2,128]{4,3,2,1,0:T(2,128)(2,1)}, u32[]{:S(2)}, u32[]{:S(2)}) collective-permute-start(bf16[1,4,128,2,128]{4,3,2,1,0:T(2,128)(2,1)} %shard_map.51), channel_id=1, source_target_pairs={{0,16},{1,17},{2,18},{3,19},{4,20},{5,21},{6,22},{7,23},{8,24},{9,... | collective-permute-start | bytes 786440 | tf_op jit(solution)/shard_map/ppermute | solution.py:20
  19.4 29.7 %collective-permute-start.6 = (bf16[2,4,128,256]{3,2,1,0:T(8,128)(2,1)S(1)}, bf16[2,4,128,256]{3,2,1,0:T(8,128)(2,1)S(1)}, u32[]{:S(2)}, u32[]{:S(2)}) collective-permute-start(bf16[2,4,128,256]{3,2,1,0:T(8,128)(2,1)S(1)} %shard_map.49.refs_2_.refs_6_.own), channel_id=1, source_target_pairs={{0,1},{1,0},{2,3},{3,2},{4,5},{5,4},{6,7},{7,6},{8,9},{9,8},{10,11... | collective-permute-start | bytes 1572872 | tf_op jit(solution)/shard_map/ppermute | solution.py:20
  20.7 29.9 %collective-permute-start.4 = (bf16[2,4,128,256]{3,2,1,0:T(8,128)(2,1)S(1)}, bf16[2,4,128,256]{3,2,1,0:T(8,128)(2,1)S(1)}, u32[]{:S(2)}, u32[]{:S(2)}) collective-permute-start(bf16[2,4,128,256]{3,2,1,0:T(8,128)(2,1)S(1)} %shard_map.47.refs_0_.refs_4_), channel_id=1, source_target_pairs={{0,1},{1,0},{2,3},{3,2},{4,5},{5,4},{6,7},{7,6},{8,9},{9,8},{10,11... | collective-permute-start | bytes 1572872 | tf_op jit(solution)/shard_map/ppermute | solution.py:20
  21.4 29.2 %collective-permute-start.5 = (bf16[2,4,128,256]{3,2,1,0:T(8,128)(2,1)S(1)}, bf16[2,4,128,256]{3,2,1,0:T(8,128)(2,1)S(1)}, u32[]{:S(2)}, u32[]{:S(2)}) collective-permute-start(bf16[2,4,128,256]{3,2,1,0:T(8,128)(2,1)S(1)} %shard_map.48.refs_1_.refs_5_), channel_id=1, source_target_pairs={{0,1},{1,0},{2,3},{3,2},{4,5},{5,4},{6,7},{7,6},{8,9},{9,8},{10,11... | collective-permute-start | bytes 1572872 | tf_op jit(solution)/shard_map/ppermute | solution.py:20
  26.1 37.5 %collective-permute-start.7 = (bf16[2,4,128,256]{3,2,1,0:T(8,128)(2,1)S(1)}, bf16[2,4,128,256]{3,2,1,0:T(8,128)(2,1)S(1)}, u32[]{:S(2)}, u32[]{:S(2)}) collective-permute-start(bf16[2,4,128,256]{3,2,1,0:T(8,128)(2,1)S(1)} %shard_map.52.refs_3_.refs_7_), channel_id=1, source_target_pairs={{0,1},{1,0},{2,3},{3,2},{4,5},{5,4},{6,7},{7,6},{8,9},{9,8},{10,11... | collective-permute-start | bytes 1572872 | tf_op jit(solution)/shard_map/ppermute | solution.py:20
  27.0 1.3 %collective-permute-start.8 = (bf16[2,64,128]{2,1,0:T(8,128)(2,1)S(1)}, bf16[2,64,128]{2,1,0:T(8,128)(2,1)S(1)}, u32[]{:S(2)}, u32[]{:S(2)}) collective-permute-start(bf16[2,64,128]{2,1,0:T(8,128)(2,1)S(1)} %bitcast.17), channel_id=1, source_target_pairs={{0,1},{1,0},{2,3},{3,2},{4,5},{5,4},{6,7},{7,6},{8,9},{9,8},{10,11... | collective-permute-start | bytes 98312 | tf_op jit(solution)/shard_map/ppermute | solution.py:20
  28.3 6.3 %collective-permute-start.11 = (bf16[2,2,64,128]{3,2,1,0:T(8,128)(2,1)S(1)}, bf16[2,2,64,128]{3,2,1,0:T(8,128)(2,1)S(1)}, u32[]{:S(2)}, u32[]{:S(2)}) collective-permute-start(bf16[2,2,64,128]{3,2,1,0:T(8,128)(2,1)S(1)} %shard_map.54.refs_0_.free_ref), channel_id=1, source_target_pairs={{0,6},{1,7},{2,4},{3,5},{4,2},{5,3},{6,0},{7,1},{8,14},{9,15},{10,... | collective-permute-start | bytes 196616 | tf_op jit(solution)/shard_map/ppermute | solution.py:20
  34.6 5.9 %collective-permute-start.10 = (bf16[2,2,64,128]{3,2,1,0:T(8,128)(2,1)S(1)}, bf16[2,2,64,128]{3,2,1,0:T(8,128)(2,1)S(1)}, u32[]{:S(2)}, u32[]{:S(2)}) collective-permute-start(bf16[2,2,64,128]{3,2,1,0:T(8,128)(2,1)S(1)} %shard_map.54.refs_0_.free_ref), channel_id=1, source_target_pairs={{0,4},{1,5},{2,6},{3,7},{4,0},{5,1},{6,2},{7,3},{8,12},{9,13},{10,... | collective-permute-start | bytes 196616 | tf_op jit(solution)/shard_map/ppermute | solution.py:20
  40.5 4.3 %collective-permute-start.9 = (bf16[2,2,64,128]{3,2,1,0:T(8,128)(2,1)S(1)}, bf16[2,2,64,128]{3,2,1,0:T(8,128)(2,1)S(1)}, u32[]{:S(2)}, u32[]{:S(2)}) collective-permute-start(bf16[2,2,64,128]{3,2,1,0:T(8,128)(2,1)S(1)} %shard_map.54.refs_0_.free_ref), channel_id=1, source_target_pairs={{0,2},{1,3},{2,0},{3,1},{4,6},{5,7},{6,4},{7,5},{8,10},{9,11},{10,... | collective-permute-start | bytes 196616 | tf_op jit(solution)/shard_map/ppermute | solution.py:20
  44.8 4.3 %collective-permute-start.12 = (bf16[2,2,64,128]{3,2,1,0:T(8,128)(2,1)S(1)}, bf16[2,2,64,128]{3,2,1,0:T(8,128)(2,1)S(1)}, u32[]{:S(2)}, u32[]{:S(2)}) collective-permute-start(bf16[2,2,64,128]{3,2,1,0:T(8,128)(2,1)S(1)} %shard_map.56), channel_id=1, source_target_pairs={{0,8},{1,9},{2,10},{3,11},{4,12},{5,13},{6,14},{7,15},{8,0},{9,1},... | collective-permute-start | bytes 196616 | tf_op jit(solution)/shard_map/ppermute | solution.py:20
  49.4 4.3 %collective-permute-start.13 = (bf16[2,2,32,256]{3,2,1,0:T(8,128)(2,1)S(1)}, bf16[2,2,32,256]{3,2,1,0:T(8,128)(2,1)S(1)}, u32[]{:S(2)}, u32[]{:S(2)}) collective-permute-start(bf16[2,2,32,256]{3,2,1,0:T(8,128)(2,1)S(1)} %shard_map.57), channel_id=1, source_target_pairs={{0,8},{1,9},{2,10},{3,11},{4,12},{5,13},{6,14},{7,15},{8,0},{9,1},... | collective-permute-start | bytes 196616 | tf_op jit(solution)/shard_map/ppermute | solution.py:20
  53.7 6.1 %collective-permute-start.16 = (bf16[2,2,64,128]{3,2,1,0:T(8,128)(2,1)S(1)}, bf16[2,2,64,128]{3,2,1,0:T(8,128)(2,1)S(1)}, u32[]{:S(2)}, u32[]{:S(2)}) collective-permute-start(bf16[2,2,64,128]{3,2,1,0:T(8,128)(2,1)S(1)} %shard_map.58.refs_0_), channel_id=1, source_target_pairs={{0,6},{1,7},{2,4},{3,5},{4,2},{5,3},{6,0},{7,1},{8,14},{9,15},{10,... | collective-permute-start | bytes 196616 | tf_op jit(solution)/shard_map/ppermute | solution.py:20
  57.2 6.4 %collective-permute-start.15 = (bf16[2,2,64,128]{3,2,1,0:T(8,128)(2,1)S(1)}, bf16[2,2,64,128]{3,2,1,0:T(8,128)(2,1)S(1)}, u32[]{:S(2)}, u32[]{:S(2)}) collective-permute-start(bf16[2,2,64,128]{3,2,1,0:T(8,128)(2,1)S(1)} %shard_map.58.refs_0_), channel_id=1, source_target_pairs={{0,4},{1,5},{2,6},{3,7},{4,0},{5,1},{6,2},{7,3},{8,12},{9,13},{10,... | collective-permute-start | bytes 196616 | tf_op jit(solution)/shard_map/ppermute | solution.py:20
  57.2 6.4 %collective-permute-start.14 = (bf16[2,2,64,128]{3,2,1,0:T(8,128)(2,1)S(1)}, bf16[2,2,64,128]{3,2,1,0:T(8,128)(2,1)S(1)}, u32[]{:S(2)}, u32[]{:S(2)}) collective-permute-start(bf16[2,2,64,128]{3,2,1,0:T(8,128)(2,1)S(1)} %shard_map.58.refs_0_), channel_id=1, source_target_pairs={{0,2},{1,3},{2,0},{3,1},{4,6},{5,7},{6,4},{7,5},{8,10},{9,11},{10,... | collective-permute-start | bytes 196616 | tf_op jit(solution)/shard_map/ppermute | solution.py:20
  64.6 6.2 %collective-permute-start.19 = (bf16[2,2,64,128]{3,2,1,0:T(8,128)(2,1)S(1)}, bf16[2,2,64,128]{3,2,1,0:T(8,128)(2,1)S(1)}, u32[]{:S(2)}, u32[]{:S(2)}) collective-permute-start(bf16[2,2,64,128]{3,2,1,0:T(8,128)(2,1)S(1)} %shard_map.59.refs_0_), channel_id=1, source_target_pairs={{0,6},{1,7},{2,4},{3,5},{4,2},{5,3},{6,0},{7,1},{8,14},{9,15},{10,... | collective-permute-start | bytes 196616 | tf_op jit(solution)/shard_map/ppermute | solution.py:20
  66.4 5.7 %collective-permute-start.18 = (bf16[2,2,64,128]{3,2,1,0:T(8,128)(2,1)S(1)}, bf16[2,2,64,128]{3,2,1,0:T(8,128)(2,1)S(1)}, u32[]{:S(2)}, u32[]{:S(2)}) collective-permute-start(bf16[2,2,64,128]{3,2,1,0:T(8,128)(2,1)S(1)} %shard_map.59.refs_0_), channel_id=1, source_target_pairs={{0,2},{1,3},{2,0},{3,1},{4,6},{5,7},{6,4},{7,5},{8,10},{9,11},{10,... | collective-permute-start | bytes 196616 | tf_op jit(solution)/shard_map/ppermute | solution.py:20
  66.4 6.4 %collective-permute-start.17 = (bf16[2,2,64,128]{3,2,1,0:T(8,128)(2,1)S(1)}, bf16[2,2,64,128]{3,2,1,0:T(8,128)(2,1)S(1)}, u32[]{:S(2)}, u32[]{:S(2)}) collective-permute-start(bf16[2,2,64,128]{3,2,1,0:T(8,128)(2,1)S(1)} %shard_map.59.refs_0_), channel_id=1, source_target_pairs={{0,4},{1,5},{2,6},{3,7},{4,0},{5,1},{6,2},{7,3},{8,12},{9,13},{10,... | collective-permute-start | bytes 196616 | tf_op jit(solution)/shard_map/ppermute | solution.py:20
  73.0 1.3 %collective-permute-start.20 = (bf16[2,64,128]{2,1,0:T(8,128)(2,1)S(1)}, bf16[2,64,128]{2,1,0:T(8,128)(2,1)S(1)}, u32[]{:S(2)}, u32[]{:S(2)}) collective-permute-start(bf16[2,64,128]{2,1,0:T(8,128)(2,1)S(1)} %shard_map.62), channel_id=1, source_target_pairs={{0,1},{1,0},{2,3},{3,2},{4,5},{5,4},{6,7},{7,6},{8,9},{9,8},{10,11... | collective-permute-start | bytes 98312 | tf_op jit(solution)/shard_map/ppermute | solution.py:20
  74.3 5.2 %collective-permute-start.23 = (bf16[2,2,64,128]{3,2,1,0:T(8,128)(2,1)S(1)}, bf16[2,2,64,128]{3,2,1,0:T(8,128)(2,1)S(1)}, u32[]{:S(2)}, u32[]{:S(2)}) collective-permute-start(bf16[2,2,64,128]{3,2,1,0:T(8,128)(2,1)S(1)} %shard_map.63.refs_0_), channel_id=1, source_target_pairs={{0,24},{1,25},{2,26},{3,27},{4,28},{5,29},{6,30},{7,31},{8,16},{9,... | collective-permute-start | bytes 196616 | tf_op jit(solution)/shard_map/ppermute | solution.py:20
  75.8 5.0 %collective-permute-start.22 = (bf16[2,2,64,128]{3,2,1,0:T(8,128)(2,1)S(1)}, bf16[2,2,64,128]{3,2,1,0:T(8,128)(2,1)S(1)}, u32[]{:S(2)}, u32[]{:S(2)}) collective-permute-start(bf16[2,2,64,128]{3,2,1,0:T(8,128)(2,1)S(1)} %shard_map.63.refs_0_), channel_id=1, source_target_pairs={{0,16},{1,17},{2,18},{3,19},{4,20},{5,21},{6,22},{7,23},{8,24},{9,... | collective-permute-start | bytes 196616 | tf_op jit(solution)/shard_map/ppermute | solution.py:20
  76.9 4.3 %collective-permute-start.21 = (bf16[2,2,64,128]{3,2,1,0:T(8,128)(2,1)S(1)}, bf16[2,2,64,128]{3,2,1,0:T(8,128)(2,1)S(1)}, u32[]{:S(2)}, u32[]{:S(2)}) collective-permute-start(bf16[2,2,64,128]{3,2,1,0:T(8,128)(2,1)S(1)} %shard_map.63.refs_0_), channel_id=1, source_target_pairs={{0,8},{1,9},{2,10},{3,11},{4,12},{5,13},{6,14},{7,15},{8,0},{9,1},... | collective-permute-start | bytes 196616 | tf_op jit(solution)/shard_map/ppermute | solution.py:20
  (2 other events, 47.6 us)

commit v4 on v3

--- a/solution.py
+++ b/solution.py
@@ -81,13 +81,15 @@
         out_ref[s] = weight
 
 
-def put_sigma(tile, b, dims, live_ref, wide, sig):
+def put_sigma(tile, b, dims, live_ref, wide, sig, scale=None):
     row_count, orb_rows, cols, lanes = dims
     rows = row_count * orb_rows
     for p in range(2):
         wide[p] = tile[p].astype(jnp.float32)
     for c in range(cols):
         weight = live_ref[b * cols + c]
+        if scale is not None:
+            weight = weight * scale
         real = wide[0, pl.ds(c, rows, stride=cols), :]
         imag = wide[1, pl.ds(c, rows, stride=cols), :]
         modulus = real * real + imag * imag
@@ -161,29 +163,23 @@
             out_ref[e, p] = update(free_ref[e, p], value, dims, wide.at[e], p).astype(out_ref.dtype)
 
 
-def step_kernel(dims, count, n_mem, live_ref, free_ref, *refs):
-    blocks, hists, (out_ref, wide, sig) = refs[:count], refs[count:-3], refs[-3:]
-    masks = [lax.axis_index("mem") ^ q for q in range(n_mem)]
-    for e, value in enumerate(integral(all_tiles(blocks), hists, masks, dims, live_ref, wide, sig)):
-        for p in range(2):
-            out_ref[e, p] = update(free_ref[e, p], value[p], dims, wide.at[e], p).astype(out_ref.dtype)
-
-
-def collect_kernel(*refs):
+def collect_kernel(masks, *refs):
     hists, out_ref = refs[:-1], refs[-1]
     count = len(hists) // 2
     for e in range(2):
-        for k in range(count):
-            out_ref[e, lax.axis_index("mem") ^ k] = hists[e * count + k][...]
-
-
-def block_integral(sums, block, k, pairs, dims, live_ref, hist_ref, wide, sig):
+        for k in range(out_ref.shape[1]):
+            i = masks.index(k) if k in masks else 0
+            out_ref[e, lax.axis_index("mem") ^ k] = hists[e * count + i][...]
+
+
+def block_integral(sums, block, k, pairs, dims, live_ref, hist_ref, wide, sig, missing=None):
     tt = lax.axis_index("tt")
     chip, core = (tt // 2) ^ k, tt % 2
     cols = dims[2]
+    scale = None if missing is None else jnp.where(chip == missing, 0.0, 1.0)
     for e in range(2):
         h = core ^ e
-        put_sigma(block.at[e], 2 * chip + h, dims, live_ref, wide.at[2 * k + e], sig.at[2 * k + e])
+        put_sigma(block.at[e], 2 * chip + h, dims, live_ref, wide.at[2 * k + e], sig.at[2 * k + e], scale)
         for i, pair in enumerate(pairs):
             at = pl.ds(h * cols, cols)
             sums[i] = tuple(
@@ -198,15 +194,38 @@
     return sums
 
 
-def early_kernel(dims, early, live_ref, hist_ref, *refs):
+def early_kernel(dims, early, last, live_ref, hist_ref, *refs):
     blocks, (out_ref, wide, sig) = refs[:-3], refs[-3:]
     zero = jnp.zeros((2 * dims[0] * dims[1], dims[2] * dims[3]), jnp.float32)
     sums = [(zero, zero), (zero, zero)]
+    missing = None if last is None else lax.axis_index("mem") ^ last
     for k, block in zip(early, blocks):
-        sums = block_integral(sums, block, k, (0, 1), dims, live_ref, hist_ref, wide, sig)
+        sums = block_integral(sums, block, k, (0, 1), dims, live_ref, hist_ref, wide, sig, missing)
     for e in range(2):
         for p, value in enumerate(as_complex(sums[e])):
             out_ref[e, p] = value
+
+
+def rest_kernel(dims, late, last, live_ref, hist_ref, own, pair, sum_ref, free_ref, *refs):
+    blocks, (out_ref, wide, sig) = refs[:-3], refs[-3:]
+    count = 2 * len(blocks)
+    mem, tt = lax.axis_index("mem"), lax.axis_index("tt")
+    missing = mem ^ last
+    for k, block in enumerate(blocks):
+        @pl.when((tt // 2) ^ k == missing)
+        def _():
+            for h in range(2):
+                e = (tt % 2) ^ h
+                put_sigma(block.at[e], 2 * missing + h, dims, live_ref, wide.at[count + h], sig.at[count + h])
+    zero = jnp.zeros((2 * dims[0] * dims[1], dims[2] * dims[3]), jnp.float32)
+    sums = [(zero, zero), (zero, zero)]
+    for h in range(2):
+        sums = [accumulate(t, sig[count + h], hist, h, dims[2]) for t, hist in zip(sums, (own, pair))]
+    sums = block_integral(sums, blocks[late], late, (0, 1), dims, live_ref, hist_ref, wide, sig, missing)
+    for e in range(2):
+        for p, value in enumerate(as_complex(sums[e])):
+            new = update(free_ref[e, p], sum_ref[e, p] + value, dims, wide.at[e], p)
+            out_ref[e, p] = new.astype(out_ref.dtype)
 
 
 def late_kernel(dims, late, pair, live_ref, hist_ref, block, sum_ref, free_ref, out_ref, wide, sig):
@@ -325,20 +344,32 @@
     blocks = gather_current(current)
     split[last] = split_history(parts_of(last))
     pair[last] = swap(split[last], 0, 1)
-    hists = [split[k] for k in range(n_mem)] + [pair[k] for k in range(n_mem)]
+    late = n_tt // 4
+    early = tuple(k for k in range(n_tt // 2) if k != late)
+
+    def collect(masks):
+        shape = (2, n_mem, *split[0].shape)
+        picked = [h[k] for h in (split, pair) for k in masks]
+        return call(functools.partial(collect_kernel, masks), (shape, bf16), picked)
+
+    some = collect(near)
     for _ in range(1, ITERS - 1):
-        current = call(
-            functools.partial(step_kernel, dims, len(blocks), n_mem),
-            (free.shape, bf16),
-            [live, free, *blocks, *hists],
+        early_sum = call(
+            functools.partial(early_kernel, dims, early, last),
+            ((2, parts, rows, cols * lanes), f32),
+            [live, some, *(blocks[k] for k in early)],
             scratch(n_tt),
         )
+        current = call(
+            functools.partial(rest_kernel, dims, late, last),
+            (free.shape, bf16),
+            [live, some, split[last], pair[last], early_sum, free, *blocks],
+            scratch(n_tt + 2),
+        )
         blocks = gather_current(current)
-    late = n_tt // 4
-    early = tuple(k for k in range(n_tt // 2) if k != late)
-    ordered = call(collect_kernel, ((2, n_mem, *hists[0].shape), bf16), hists)
+    ordered = collect(tuple(range(n_mem)))
     early_sum = call(
-        functools.partial(early_kernel, dims, early),
+        functools.partial(early_kernel, dims, early, None),
         ((2, parts, rows, cols * lanes), f32),
         [live, ordered, *(blocks[k] for k in early)],
         scratch(n_tt),

time: 82.2 us -> 84.4 us (1.027)
  waiting for transfers between devices: 43.4 us -> 45 us
    ppermute x24, waiting for transfers between devices: 43.4 us -> 45 us  [swap(): return lax.ppermute(value, BOTH, pairs)]
    pallas_call x19 -> x21, Pallas kernels: 7.36 us -> 7.89 us  [call(): pl.pallas_call(kernel, out_shape=[jax.ShapeDtypeStruct(s, d) for s, d in...]
  transfers between devices with their start and end apart: 24 -> 24, of which waited for: 17 -> 18; matrix products, arithmetic and copies ran while one was open for 1% -> 1% of each run, Pallas kernels for 7% -> 8%
where the time goes in v4:
time: 84.4 us; the launch traced here: 84.2 us
  waiting for transfers between devices  45 us (53%)
  starting transfers between devices  28.7 us (34%)
  Pallas kernels  7.89 us (9%)
  local copies, waits for them, and re-layouts  1.84 us (2%)
    ppermute x24, waiting for transfers between devices, swap(): return lax.ppermute(value, BOTH, pairs)  45 us
    ppermute x24, starting transfers between devices, swap(): return lax.ppermute(value, BOTH, pairs)  28.7 us
    pallas_call x21, Pallas kernels, call(): pl.pallas_call(kernel, out_shape=[jax.ShapeDtypeStruct(s, d) for s, d in...  7.89 us
  transfers between devices with their start and end apart: 24, of which 18 were waited for; matrix products, arithmetic and copies ran while one was open for 1% of the time, Pallas kernels for 8%

profile of v4, /device:TPU:0, one launch (start us, length us, event | category | flops | bytes accessed | tf_op | source)
XLA Modules:
  0.0 84.2 jit_solution(16271997820136049735)
XLA Ops:
  0.0 3.0 %collective-permute-start.1 = (bf16[2,4,128,2,128]{4,3,2,1,0:T(2,128)(2,1)}, bf16[2,4,128,2,128]{4,3,2,1,0:T(2,128)(2,1)S(1)}, u32[]{:S(2)}, u32[]{:S(2)}) collective-permute-start(bf16[2,4,128,2,128]{4,3,2,1,0:T(2,128)(2,1)} %param.4), channel_id=1, source_target_pairs={{0,16},{1,17},{2,18},{3,19},{4,20},{5,21},{6,22},{7,23},{8,24},{9,... | collective-permute-start | bytes 1572872 | tf_op jit(solution)/shard_map/ppermute | solution.py:20
  3.0 1.5 %collective-permute-start = (bf16[2,4,128,2,128]{4,3,2,1,0:T(2,128)(2,1)}, bf16[2,4,128,2,128]{4,3,2,1,0:T(2,128)(2,1)S(1)}, u32[]{:S(2)}, u32[]{:S(2)}) collective-permute-start(bf16[2,4,128,2,128]{4,3,2,1,0:T(2,128)(2,1)} %param.4), channel_id=1, source_target_pairs={{0,8},{1,9},{2,10},{3,11},{4,12},{5,13},{6,14},{7,15},{8,0},{9,1},... | collective-permute-start | bytes 1572872 | tf_op jit(solution)/shard_map/ppermute | solution.py:20
  4.5 10.6 %collective-permute-done.1.ref = bf16[2,4,128,2,128]{4,3,2,1,0:T(2,128)(2,1)S(1)} collective-permute-done((bf16[2,4,128,2,128]{4,3,2,1,0:T(2,128)(2,1)}, bf16[2,4,128,2,128]{4,3,2,1,0:T(2,128)(2,1)S(1)}, u32[]{:S(2)}, u32[]{:S(2)}) %collective-permute-start.1) | collective-permute-done | bytes 524320 | tf_op jit(solution)/shard_map/ppermute | solution.py:20
  15.2 1.8 %collective-permute-start.2 = (bf16[1,4,128,2,128]{4,3,2,1,0:T(2,128)(2,1)S(1)}, bf16[1,4,128,2,128]{4,3,2,1,0:T(2,128)(2,1)}, u32[]{:S(2)}, u32[]{:S(2)}) collective-permute-start(bf16[1,4,128,2,128]{4,3,2,1,0:T(2,128)(2,1)S(1)} %shard_map.50), channel_id=1, source_target_pairs={{0,8},{1,9},{2,10},{3,11},{4,12},{5,13},{6,14},{7,15},{8,0},{9,1},... | collective-permute-start | bytes 786440 | tf_op jit(solution)/shard_map/ppermute | solution.py:20
  17.7 1.5 %collective-permute-start.3 = (bf16[1,4,128,2,128]{4,3,2,1,0:T(2,128)(2,1)}, bf16[1,4,128,2,128]{4,3,2,1,0:T(2,128)(2,1)}, u32[]{:S(2)}, u32[]{:S(2)}) collective-permute-start(bf16[1,4,128,2,128]{4,3,2,1,0:T(2,128)(2,1)} %shard_map.51), channel_id=1, source_target_pairs={{0,16},{1,17},{2,18},{3,19},{4,20},{5,21},{6,22},{7,23},{8,24},{9,... | collective-permute-start | bytes 786440 | tf_op jit(solution)/shard_map/ppermute | solution.py:20
  21.5 1.3 %collective-permute-done.2 = bf16[1,4,128,2,128]{4,3,2,1,0:T(2,128)(2,1)} collective-permute-done((bf16[1,4,128,2,128]{4,3,2,1,0:T(2,128)(2,1)S(1)}, bf16[1,4,128,2,128]{4,3,2,1,0:T(2,128)(2,1)}, u32[]{:S(2)}, u32[]{:S(2)}) %collective-permute-start.2) | collective-permute-done | bytes 262176 | tf_op jit(solution)/shard_map/ppermute | solution.py:20
  22.8 2.1 %collective-permute-done.3 = bf16[1,4,128,2,128]{4,3,2,1,0:T(2,128)(2,1)} collective-permute-done((bf16[1,4,128,2,128]{4,3,2,1,0:T(2,128)(2,1)}, bf16[1,4,128,2,128]{4,3,2,1,0:T(2,128)(2,1)}, u32[]{:S(2)}, u32[]{:S(2)}) %collective-permute-start.3) | collective-permute-done | bytes 262176 | tf_op jit(solution)/shard_map/ppermute | solution.py:20
  24.9 1.2 %shard_map.52.refs_3_.own = bf16[2,4,128,256]{3,2,1,0:T(8,128)(2,1)S(1)} custom-call(bf16[1,4,256,128]{3,2,1,0:T(8,128)(2,1)} %bitcast.3.refs_0_, bf16[1,4,256,128]{3,2,1,0:T(8,128)(2,1)} %bitcast.4.refs_1_), custom_call_target="tpu_custom_call" | custom-call | tf_op jit(solution)/shard_map/pallas_call | solution.py:27
  28.3 2.6 %collective-permute-start.10 = (bf16[2,2,64,128]{3,2,1,0:T(8,128)(2,1)S(1)}, bf16[2,2,64,128]{3,2,1,0:T(8,128)(2,1)S(1)}, u32[]{:S(2)}, u32[]{:S(2)}) collective-permute-start(bf16[2,2,64,128]{3,2,1,0:T(8,128)(2,1)S(1)} %shard_map.55.refs_0_.free_ref), channel_id=1, source_target_pairs={{0,4},{1,5},{2,6},{3,7},{4,0},{5,1},{6,2},{7,3},{8,12},{9,13},{10,... | collective-permute-start | bytes 196616 | tf_op jit(solution)/shard_map/ppermute | solution.py:20
  30.9 4.1 %collective-permute-done.10.refs_2_ = bf16[2,2,64,128]{3,2,1,0:T(8,128)(2,1)S(1)} collective-permute-done((bf16[2,2,64,128]{3,2,1,0:T(8,128)(2,1)S(1)}, bf16[2,2,64,128]{3,2,1,0:T(8,128)(2,1)S(1)}, u32[]{:S(2)}, u32[]{:S(2)}) %collective-permute-start.10) | collective-permute-done | bytes 65568 | tf_op jit(solution)/shard_map/ppermute | solution.py:20
  35.0 3.5 %collective-permute-start.11 = (bf16[2,2,64,128]{3,2,1,0:T(8,128)(2,1)S(1)}, bf16[2,2,64,128]{3,2,1,0:T(8,128)(2,1)S(1)}, u32[]{:S(2)}, u32[]{:S(2)}) collective-permute-start(bf16[2,2,64,128]{3,2,1,0:T(8,128)(2,1)S(1)} %shard_map.55.refs_0_.free_ref), channel_id=1, source_target_pairs={{0,6},{1,7},{2,4},{3,5},{4,2},{5,3},{6,0},{7,1},{8,14},{9,15},{10,... | collective-permute-start | bytes 196616 | tf_op jit(solution)/shard_map/ppermute | solution.py:20
  38.5 2.6 %collective-permute-done.11.refs_3_ = bf16[2,2,64,128]{3,2,1,0:T(8,128)(2,1)S(1)} collective-permute-done((bf16[2,2,64,128]{3,2,1,0:T(8,128)(2,1)S(1)}, bf16[2,2,64,128]{3,2,1,0:T(8,128)(2,1)S(1)}, u32[]{:S(2)}, u32[]{:S(2)}) %collective-permute-start.11) | collective-permute-done | bytes 65568 | tf_op jit(solution)/shard_map/ppermute | solution.py:20
  41.0 4.3 %collective-permute-done.9.refs_1_ = bf16[2,2,64,128]{3,2,1,0:T(8,128)(2,1)S(1)} collective-permute-done((bf16[2,2,64,128]{3,2,1,0:T(8,128)(2,1)S(1)}, bf16[2,2,64,128]{3,2,1,0:T(8,128)(2,1)S(1)}, u32[]{:S(2)}, u32[]{:S(2)}) %collective-permute-start.9) | collective-permute-done | bytes 65568 | tf_op jit(solution)/shard_map/ppermute | solution.py:20
  47.7 2.3 %collective-permute-done.12.tile_ref = bf16[2,2,64,128]{3,2,1,0:T(8,128)(2,1)S(1)} collective-permute-done((bf16[2,2,64,128]{3,2,1,0:T(8,128)(2,1)S(1)}, bf16[2,2,64,128]{3,2,1,0:T(8,128)(2,1)S(1)}, u32[]{:S(2)}, u32[]{:S(2)}) %collective-permute-start.12) | collective-permute-done | bytes 65568 | tf_op jit(solution)/shard_map/ppermute | solution.py:20
  50.4 1.2 %collective-permute-start.13 = (bf16[2,2,32,256]{3,2,1,0:T(8,128)(2,1)S(1)}, bf16[2,2,32,256]{3,2,1,0:T(8,128)(2,1)S(1)}, u32[]{:S(2)}, u32[]{:S(2)}) collective-permute-start(bf16[2,2,32,256]{3,2,1,0:T(8,128)(2,1)S(1)} %shard_map.58), channel_id=1, source_target_pairs={{0,8},{1,9},{2,10},{3,11},{4,12},{5,13},{6,14},{7,15},{8,0},{9,1},... | collective-permute-start | bytes 196616 | tf_op jit(solution)/shard_map/ppermute | solution.py:20
  52.4 2.3 %collective-permute-done.13.far_ref = bf16[2,2,32,256]{3,2,1,0:T(8,128)(2,1)S(1)} collective-permute-done((bf16[2,2,32,256]{3,2,1,0:T(8,128)(2,1)S(1)}, bf16[2,2,32,256]{3,2,1,0:T(8,128)(2,1)S(1)}, u32[]{:S(2)}, u32[]{:S(2)}) %collective-permute-start.13) | collective-permute-done | bytes 65568 | tf_op jit(solution)/shard_map/ppermute | solution.py:20
  54.8 3.5 %collective-permute-start.15 = (bf16[2,2,64,128]{3,2,1,0:T(8,128)(2,1)S(1)}, bf16[2,2,64,128]{3,2,1,0:T(8,128)(2,1)S(1)}, u32[]{:S(2)}, u32[]{:S(2)}) collective-permute-start(bf16[2,2,64,128]{3,2,1,0:T(8,128)(2,1)S(1)} %shard_map.59.refs_0_), channel_id=1, source_target_pairs={{0,6},{1,7},{2,4},{3,5},{4,2},{5,3},{6,0},{7,1},{8,14},{9,15},{10,... | collective-permute-start | bytes 196616 | tf_op jit(solution)/shard_map/ppermute | solution.py:20
  59.1 2.2 %collective-permute-done.15.refs_2_.refs_3_ = bf16[2,2,64,128]{3,2,1,0:T(8,128)(2,1)S(1)} collective-permute-done((bf16[2,2,64,128]{3,2,1,0:T(8,128)(2,1)S(1)}, bf16[2,2,64,128]{3,2,1,0:T(8,128)(2,1)S(1)}, u32[]{:S(2)}, u32[]{:S(2)}) %collective-permute-start.15) | collective-permute-done | bytes 65568 | tf_op jit(solution)/shard_map/ppermute | solution.py:20
  62.0 4.3 %collective-permute-done.16.refs_2_ = bf16[2,2,64,128]{3,2,1,0:T(8,128)(2,1)S(1)} collective-permute-done((bf16[2,2,64,128]{3,2,1,0:T(8,128)(2,1)S(1)}, bf16[2,2,64,128]{3,2,1,0:T(8,128)(2,1)S(1)}, u32[]{:S(2)}, u32[]{:S(2)}) %collective-permute-start.16) | collective-permute-done | bytes 65568 | tf_op jit(solution)/shard_map/ppermute | solution.py:20
  66.9 1.8 %collective-permute-start.19 = (bf16[2,2,64,128]{3,2,1,0:T(8,128)(2,1)S(1)}, bf16[2,2,64,128]{3,2,1,0:T(8,128)(2,1)S(1)}, u32[]{:S(2)}, u32[]{:S(2)}) collective-permute-start(bf16[2,2,64,128]{3,2,1,0:T(8,128)(2,1)S(1)} %shard_map.61.refs_0_), channel_id=1, source_target_pairs={{0,6},{1,7},{2,4},{3,5},{4,2},{5,3},{6,0},{7,1},{8,14},{9,15},{10,... | collective-permute-start | bytes 196616 | tf_op jit(solution)/shard_map/ppermute | solution.py:20
  68.7 1.6 %collective-permute-start.17 = (bf16[2,2,64,128]{3,2,1,0:T(8,128)(2,1)S(1)}, bf16[2,2,64,128]{3,2,1,0:T(8,128)(2,1)S(1)}, u32[]{:S(2)}, u32[]{:S(2)}) collective-permute-start(bf16[2,2,64,128]{3,2,1,0:T(8,128)(2,1)S(1)} %shard_map.61.refs_0_), channel_id=1, source_target_pairs={{0,4},{1,5},{2,6},{3,7},{4,0},{5,1},{6,2},{7,3},{8,12},{9,13},{10,... | collective-permute-start | bytes 196616 | tf_op jit(solution)/shard_map/ppermute | solution.py:20
  71.2 2.0 %collective-permute-done.19.refs_2_ = bf16[2,2,64,128]{3,2,1,0:T(8,128)(2,1)S(1)} collective-permute-done((bf16[2,2,64,128]{3,2,1,0:T(8,128)(2,1)S(1)}, bf16[2,2,64,128]{3,2,1,0:T(8,128)(2,1)S(1)}, u32[]{:S(2)}, u32[]{:S(2)}) %collective-permute-start.19) | collective-permute-done | bytes 65568 | tf_op jit(solution)/shard_map/ppermute | solution.py:20
  78.3 1.4 %collective-permute-start.23 = (bf16[2,2,64,128]{3,2,1,0:T(8,128)(2,1)S(1)}, bf16[2,2,64,128]{3,2,1,0:T(8,128)(2,1)S(1)}, u32[]{:S(2)}, u32[]{:S(2)}) collective-permute-start(bf16[2,2,64,128]{3,2,1,0:T(8,128)(2,1)S(1)} %shard_map.65.refs_0_), channel_id=1, source_target_pairs={{0,24},{1,25},{2,26},{3,27},{4,28},{5,29},{6,30},{7,31},{8,16},{9,... | collective-permute-start | bytes 196616 | tf_op jit(solution)/shard_map/ppermute | solution.py:20
  80.5 1.9 %collective-permute-done.22.refs_2_ = bf16[2,2,64,128]{3,2,1,0:T(8,128)(2,1)S(1)} collective-permute-done((bf16[2,2,64,128]{3,2,1,0:T(8,128)(2,1)S(1)}, bf16[2,2,64,128]{3,2,1,0:T(8,128)(2,1)S(1)}, u32[]{:S(2)}, u32[]{:S(2)}) %collective-permute-start.22) | collective-permute-done | bytes 65568 | tf_op jit(solution)/shard_map/ppermute | solution.py:20
  (50 shorter events, 18.8 us)
Async XLA Ops:
  0.0 15.1 %collective-permute-start.1 = (bf16[2,4,128,2,128]{4,3,2,1,0:T(2,128)(2,1)}, bf16[2,4,128,2,128]{4,3,2,1,0:T(2,128)(2,1)S(1)}, u32[]{:S(2)}, u32[]{:S(2)}) collective-permute-start(bf16[2,4,128,2,128]{4,3,2,1,0:T(2,128)(2,1)} %param.4), channel_id=1, source_target_pairs={{0,16},{1,17},{2,18},{3,19},{4,20},{5,21},{6,22},{7,23},{8,24},{9,... | collective-permute-start | bytes 1572872 | tf_op jit(solution)/shard_map/ppermute | solution.py:20
  3.0 13.9 %collective-permute-start = (bf16[2,4,128,2,128]{4,3,2,1,0:T(2,128)(2,1)}, bf16[2,4,128,2,128]{4,3,2,1,0:T(2,128)(2,1)S(1)}, u32[]{:S(2)}, u32[]{:S(2)}) collective-permute-start(bf16[2,4,128,2,128]{4,3,2,1,0:T(2,128)(2,1)} %param.4), channel_id=1, source_target_pairs={{0,8},{1,9},{2,10},{3,11},{4,12},{5,13},{6,14},{7,15},{8,0},{9,1},... | collective-permute-start | bytes 1572872 | tf_op jit(solution)/shard_map/ppermute | solution.py:20
  15.2 7.6 %collective-permute-start.2 = (bf16[1,4,128,2,128]{4,3,2,1,0:T(2,128)(2,1)S(1)}, bf16[1,4,128,2,128]{4,3,2,1,0:T(2,128)(2,1)}, u32[]{:S(2)}, u32[]{:S(2)}) collective-permute-start(bf16[1,4,128,2,128]{4,3,2,1,0:T(2,128)(2,1)S(1)} %shard_map.50), channel_id=1, source_target_pairs={{0,8},{1,9},{2,10},{3,11},{4,12},{5,13},{6,14},{7,15},{8,0},{9,1},... | collective-permute-start | bytes 786440 | tf_op jit(solution)/shard_map/ppermute | solution.py:20
  17.7 7.2 %collective-permute-start.3 = (bf16[1,4,128,2,128]{4,3,2,1,0:T(2,128)(2,1)}, bf16[1,4,128,2,128]{4,3,2,1,0:T(2,128)(2,1)}, u32[]{:S(2)}, u32[]{:S(2)}) collective-permute-start(bf16[1,4,128,2,128]{4,3,2,1,0:T(2,128)(2,1)} %shard_map.51), channel_id=1, source_target_pairs={{0,16},{1,17},{2,18},{3,19},{4,20},{5,21},{6,22},{7,23},{8,24},{9,... | collective-permute-start | bytes 786440 | tf_op jit(solution)/shard_map/ppermute | solution.py:20
  19.4 30.7 %collective-permute-start.6 = (bf16[2,4,128,256]{3,2,1,0:T(8,128)(2,1)S(1)}, bf16[2,4,128,256]{3,2,1,0:T(8,128)(2,1)S(1)}, u32[]{:S(2)}, u32[]{:S(2)}) collective-permute-start(bf16[2,4,128,256]{3,2,1,0:T(8,128)(2,1)S(1)} %shard_map.49.refs_2_.refs_6_.own), channel_id=1, source_target_pairs={{0,1},{1,0},{2,3},{3,2},{4,5},{5,4},{6,7},{7,6},{8,9},{9,8},{10,11... | collective-permute-start | bytes 1572872 | tf_op jit(solution)/shard_map/ppermute | solution.py:20
  20.7 30.9 %collective-permute-start.4 = (bf16[2,4,128,256]{3,2,1,0:T(8,128)(2,1)S(1)}, bf16[2,4,128,256]{3,2,1,0:T(8,128)(2,1)S(1)}, u32[]{:S(2)}, u32[]{:S(2)}) collective-permute-start(bf16[2,4,128,256]{3,2,1,0:T(8,128)(2,1)S(1)} %shard_map.47.refs_0_.refs_4_), channel_id=1, source_target_pairs={{0,1},{1,0},{2,3},{3,2},{4,5},{5,4},{6,7},{7,6},{8,9},{9,8},{10,11... | collective-permute-start | bytes 1572872 | tf_op jit(solution)/shard_map/ppermute | solution.py:20
  21.4 30.2 %collective-permute-start.5 = (bf16[2,4,128,256]{3,2,1,0:T(8,128)(2,1)S(1)}, bf16[2,4,128,256]{3,2,1,0:T(8,128)(2,1)S(1)}, u32[]{:S(2)}, u32[]{:S(2)}) collective-permute-start(bf16[2,4,128,256]{3,2,1,0:T(8,128)(2,1)S(1)} %shard_map.48.refs_1_.refs_5_), channel_id=1, source_target_pairs={{0,1},{1,0},{2,3},{3,2},{4,5},{5,4},{6,7},{7,6},{8,9},{9,8},{10,11... | collective-permute-start | bytes 1572872 | tf_op jit(solution)/shard_map/ppermute | solution.py:20
  26.1 40.2 %collective-permute-start.7 = (bf16[2,4,128,256]{3,2,1,0:T(8,128)(2,1)S(1)}, bf16[2,4,128,256]{3,2,1,0:T(8,128)(2,1)S(1)}, u32[]{:S(2)}, u32[]{:S(2)}) collective-permute-start(bf16[2,4,128,256]{3,2,1,0:T(8,128)(2,1)S(1)} %shard_map.52.refs_3_.own), channel_id=1, source_target_pairs={{0,1},{1,0},{2,3},{3,2},{4,5},{5,4},{6,7},{7,6},{8,9},{9,8},{10,11... | collective-permute-start | bytes 1572872 | tf_op jit(solution)/shard_map/ppermute | solution.py:20
  27.0 1.3 %collective-permute-start.8 = (bf16[2,64,128]{2,1,0:T(8,128)(2,1)S(1)}, bf16[2,64,128]{2,1,0:T(8,128)(2,1)S(1)}, u32[]{:S(2)}, u32[]{:S(2)}) collective-permute-start(bf16[2,64,128]{2,1,0:T(8,128)(2,1)S(1)} %bitcast.17), channel_id=1, source_target_pairs={{0,1},{1,0},{2,3},{3,2},{4,5},{5,4},{6,7},{7,6},{8,9},{9,8},{10,11... | collective-permute-start | bytes 98312 | tf_op jit(solution)/shard_map/ppermute | solution.py:20
  28.3 6.6 %collective-permute-start.10 = (bf16[2,2,64,128]{3,2,1,0:T(8,128)(2,1)S(1)}, bf16[2,2,64,128]{3,2,1,0:T(8,128)(2,1)S(1)}, u32[]{:S(2)}, u32[]{:S(2)}) collective-permute-start(bf16[2,2,64,128]{3,2,1,0:T(8,128)(2,1)S(1)} %shard_map.55.refs_0_.free_ref), channel_id=1, source_target_pairs={{0,4},{1,5},{2,6},{3,7},{4,0},{5,1},{6,2},{7,3},{8,12},{9,13},{10,... | collective-permute-start | bytes 196616 | tf_op jit(solution)/shard_map/ppermute | solution.py:20
  35.0 6.1 %collective-permute-start.11 = (bf16[2,2,64,128]{3,2,1,0:T(8,128)(2,1)S(1)}, bf16[2,2,64,128]{3,2,1,0:T(8,128)(2,1)S(1)}, u32[]{:S(2)}, u32[]{:S(2)}) collective-permute-start(bf16[2,2,64,128]{3,2,1,0:T(8,128)(2,1)S(1)} %shard_map.55.refs_0_.free_ref), channel_id=1, source_target_pairs={{0,6},{1,7},{2,4},{3,5},{4,2},{5,3},{6,0},{7,1},{8,14},{9,15},{10,... | collective-permute-start | bytes 196616 | tf_op jit(solution)/shard_map/ppermute | solution.py:20
  41.0 4.3 %collective-permute-start.9 = (bf16[2,2,64,128]{3,2,1,0:T(8,128)(2,1)S(1)}, bf16[2,2,64,128]{3,2,1,0:T(8,128)(2,1)S(1)}, u32[]{:S(2)}, u32[]{:S(2)}) collective-permute-start(bf16[2,2,64,128]{3,2,1,0:T(8,128)(2,1)S(1)} %shard_map.55.refs_0_.free_ref), channel_id=1, source_target_pairs={{0,2},{1,3},{2,0},{3,1},{4,6},{5,7},{6,4},{7,5},{8,10},{9,11},{10,... | collective-permute-start | bytes 196616 | tf_op jit(solution)/shard_map/ppermute | solution.py:20
  45.3 4.7 %collective-permute-start.12 = (bf16[2,2,64,128]{3,2,1,0:T(8,128)(2,1)S(1)}, bf16[2,2,64,128]{3,2,1,0:T(8,128)(2,1)S(1)}, u32[]{:S(2)}, u32[]{:S(2)}) collective-permute-start(bf16[2,2,64,128]{3,2,1,0:T(8,128)(2,1)S(1)} %shard_map.57), channel_id=1, source_target_pairs={{0,8},{1,9},{2,10},{3,11},{4,12},{5,13},{6,14},{7,15},{8,0},{9,1},... | collective-permute-start | bytes 196616 | tf_op jit(solution)/shard_map/ppermute | solution.py:20
  50.4 4.3 %collective-permute-start.13 = (bf16[2,2,32,256]{3,2,1,0:T(8,128)(2,1)S(1)}, bf16[2,2,32,256]{3,2,1,0:T(8,128)(2,1)S(1)}, u32[]{:S(2)}, u32[]{:S(2)}) collective-permute-start(bf16[2,2,32,256]{3,2,1,0:T(8,128)(2,1)S(1)} %shard_map.58), channel_id=1, source_target_pairs={{0,8},{1,9},{2,10},{3,11},{4,12},{5,13},{6,14},{7,15},{8,0},{9,1},... | collective-permute-start | bytes 196616 | tf_op jit(solution)/shard_map/ppermute | solution.py:20
  54.7 4.4 %collective-permute-start.14 = (bf16[2,2,64,128]{3,2,1,0:T(8,128)(2,1)S(1)}, bf16[2,2,64,128]{3,2,1,0:T(8,128)(2,1)S(1)}, u32[]{:S(2)}, u32[]{:S(2)}) collective-permute-start(bf16[2,2,64,128]{3,2,1,0:T(8,128)(2,1)S(1)} %shard_map.59.refs_0_), channel_id=1, source_target_pairs={{0,2},{1,3},{2,0},{3,1},{4,6},{5,7},{6,4},{7,5},{8,10},{9,11},{10,... | collective-permute-start | bytes 196616 | tf_op jit(solution)/shard_map/ppermute | solution.py:20
  54.8 6.5 %collective-permute-start.15 = (bf16[2,2,64,128]{3,2,1,0:T(8,128)(2,1)S(1)}, bf16[2,2,64,128]{3,2,1,0:T(8,128)(2,1)S(1)}, u32[]{:S(2)}, u32[]{:S(2)}) collective-permute-start(bf16[2,2,64,128]{3,2,1,0:T(8,128)(2,1)S(1)} %shard_map.59.refs_0_), channel_id=1, source_target_pairs={{0,6},{1,7},{2,4},{3,5},{4,2},{5,3},{6,0},{7,1},{8,14},{9,15},{10,... | collective-permute-start | bytes 196616 | tf_op jit(solution)/shard_map/ppermute | solution.py:20
  58.3 8.0 %collective-permute-start.16 = (bf16[2,2,64,128]{3,2,1,0:T(8,128)(2,1)S(1)}, bf16[2,2,64,128]{3,2,1,0:T(8,128)(2,1)S(1)}, u32[]{:S(2)}, u32[]{:S(2)}) collective-permute-start(bf16[2,2,64,128]{3,2,1,0:T(8,128)(2,1)S(1)} %shard_map.59.refs_0_), channel_id=1, source_target_pairs={{0,4},{1,5},{2,6},{3,7},{4,0},{5,1},{6,2},{7,3},{8,12},{9,13},{10,... | collective-permute-start | bytes 196616 | tf_op jit(solution)/shard_map/ppermute | solution.py:20
  66.8 4.3 %collective-permute-start.18 = (bf16[2,2,64,128]{3,2,1,0:T(8,128)(2,1)S(1)}, bf16[2,2,64,128]{3,2,1,0:T(8,128)(2,1)S(1)}, u32[]{:S(2)}, u32[]{:S(2)}) collective-permute-start(bf16[2,2,64,128]{3,2,1,0:T(8,128)(2,1)S(1)} %shard_map.61.refs_0_), channel_id=1, source_target_pairs={{0,2},{1,3},{2,0},{3,1},{4,6},{5,7},{6,4},{7,5},{8,10},{9,11},{10,... | collective-permute-start | bytes 196616 | tf_op jit(solution)/shard_map/ppermute | solution.py:20
  66.9 6.2 %collective-permute-start.19 = (bf16[2,2,64,128]{3,2,1,0:T(8,128)(2,1)S(1)}, bf16[2,2,64,128]{3,2,1,0:T(8,128)(2,1)S(1)}, u32[]{:S(2)}, u32[]{:S(2)}) collective-permute-start(bf16[2,2,64,128]{3,2,1,0:T(8,128)(2,1)S(1)} %shard_map.61.refs_0_), channel_id=1, source_target_pairs={{0,6},{1,7},{2,4},{3,5},{4,2},{5,3},{6,0},{7,1},{8,14},{9,15},{10,... | collective-permute-start | bytes 196616 | tf_op jit(solution)/shard_map/ppermute | solution.py:20
  68.7 6.0 %collective-permute-start.17 = (bf16[2,2,64,128]{3,2,1,0:T(8,128)(2,1)S(1)}, bf16[2,2,64,128]{3,2,1,0:T(8,128)(2,1)S(1)}, u32[]{:S(2)}, u32[]{:S(2)}) collective-permute-start(bf16[2,2,64,128]{3,2,1,0:T(8,128)(2,1)S(1)} %shard_map.61.refs_0_), channel_id=1, source_target_pairs={{0,4},{1,5},{2,6},{3,7},{4,0},{5,1},{6,2},{7,3},{8,12},{9,13},{10,... | collective-permute-start | bytes 196616 | tf_op jit(solution)/shard_map/ppermute | solution.py:20
  75.0 1.3 %collective-permute-start.20 = (bf16[2,64,128]{2,1,0:T(8,128)(2,1)S(1)}, bf16[2,64,128]{2,1,0:T(8,128)(2,1)S(1)}, u32[]{:S(2)}, u32[]{:S(2)}) collective-permute-start(bf16[2,64,128]{2,1,0:T(8,128)(2,1)S(1)} %shard_map.64), channel_id=1, source_target_pairs={{0,1},{1,0},{2,3},{3,2},{4,5},{5,4},{6,7},{7,6},{8,9},{9,8},{10,11... | collective-permute-start | bytes 98312 | tf_op jit(solution)/shard_map/ppermute | solution.py:20
  76.2 4.3 %collective-permute-start.21 = (bf16[2,2,64,128]{3,2,1,0:T(8,128)(2,1)S(1)}, bf16[2,2,64,128]{3,2,1,0:T(8,128)(2,1)S(1)}, u32[]{:S(2)}, u32[]{:S(2)}) collective-permute-start(bf16[2,2,64,128]{3,2,1,0:T(8,128)(2,1)S(1)} %shard_map.65.refs_0_), channel_id=1, source_target_pairs={{0,8},{1,9},{2,10},{3,11},{4,12},{5,13},{6,14},{7,15},{8,0},{9,1},... | collective-permute-start | bytes 196616 | tf_op jit(solution)/shard_map/ppermute | solution.py:20
  77.4 5.0 %collective-permute-start.22 = (bf16[2,2,64,128]{3,2,1,0:T(8,128)(2,1)S(1)}, bf16[2,2,64,128]{3,2,1,0:T(8,128)(2,1)S(1)}, u32[]{:S(2)}, u32[]{:S(2)}) collective-permute-start(bf16[2,2,64,128]{3,2,1,0:T(8,128)(2,1)S(1)} %shard_map.65.refs_0_), channel_id=1, source_target_pairs={{0,16},{1,17},{2,18},{3,19},{4,20},{5,21},{6,22},{7,23},{8,24},{9,... | collective-permute-start | bytes 196616 | tf_op jit(solution)/shard_map/ppermute | solution.py:20
  78.3 5.2 %collective-permute-start.23 = (bf16[2,2,64,128]{3,2,1,0:T(8,128)(2,1)S(1)}, bf16[2,2,64,128]{3,2,1,0:T(8,128)(2,1)S(1)}, u32[]{:S(2)}, u32[]{:S(2)}) collective-permute-start(bf16[2,2,64,128]{3,2,1,0:T(8,128)(2,1)S(1)} %shard_map.65.refs_0_), channel_id=1, source_target_pairs={{0,24},{1,25},{2,26},{3,27},{4,28},{5,29},{6,30},{7,31},{8,16},{9,... | collective-permute-start | bytes 196616 | tf_op jit(solution)/shard_map/ppermute | solution.py:20
  (2 other events, 48.1 us)
